TPU v7x, 32 devices: a whole 2x2x4 slice. The times are simulated.
32 devices in a mesh: enc: 2 (over y), ctx: 4 (over z), tp: 4 (over x, core).
Axes of the slice: x: 2, y: 2, z: 4, core: 2. Of those that a mesh axis runs over, the one named last changes fastest.
Arguments:
- query_rows: bfloat16 [6144, 6144], P(('enc', 'ctx', 'tp')), may hold values from -5 to 5
- key_rows: bfloat16 [6144, 6144], P(('enc', 'ctx', 'tp')), may hold values from -5 to 5
- value_rows: bfloat16 [6144, 6144], P(('enc', 'ctx', 'tp')), may hold values from -6 to 6
- out_grad: bfloat16 [6144, 6144], P(('enc', 'ctx', 'tp')), may hold values from -6 to 6
- clip_lengths: int32 [16], replicated, may hold values from 1 to 768, 6144 in all
Outputs:
- attended: bfloat16 [6144, 6144], P(('enc', 'ctx', 'tp'))
- query_grad: bfloat16 [6144, 6144], P(('enc', 'ctx', 'tp'))
- key_grad: bfloat16 [6144, 6144], P(('enc', 'ctx', 'tp'))
- value_grad: bfloat16 [6144, 6144], P(('enc', 'ctx', 'tp'))
Inputs may be any that keep to these rules, and one draw needn't show every extreme that they name: `clip_lengths`: clip lengths sum to 6144; the longest clip has exactly 768 tokens.
All inputs are finite; a program needn't handle non-finite values.
Results may differ from a plain program's by a relative error of at most 0.011.
Values may be sent and summed in bfloat16 or wider, within the bound.
A program may use at most 192 MiB of HBM per device.

v0:
```python
import jax
import jax.numpy as jnp
from jax import lax
from jax.sharding import PartitionSpec as P

DH = 128


masked_score = -1e30


def padded(cells, sides, width):
    for axis, dim in sides:
        count = lax.axis_size(axis)
        ends = count - 1
        head = lax.slice_in_dim(cells, 0, width, axis=dim)
        tail = lax.slice_in_dim(cells, cells.shape[dim] - width, cells.shape[dim], axis=dim)
        cells = jnp.concatenate(
            [
                lax.ppermute(tail, axis, [(i, (i + 1) % count) for i in range(ends)]),
                cells,
                lax.ppermute(head, axis, [((i + 1) % count, i) for i in range(ends)]),
            ],
            axis=dim,
        )
    return cells


def from_behind(block, axis, distance):
    devices = range(lax.axis_size(axis))
    route = [(i - distance, i) for i in devices if i - distance in devices]
    return lax.ppermute(block, axis, route)


def clip_numbers(positions, clip_lengths):
    clip_ends = jnp.cumsum(clip_lengths)
    return jnp.sum((positions[:, None] >= clip_ends[None, :]).astype(jnp.int32), axis=1)


def window_pass(query_block, grad_block, key_window, value_window, allowed, score_scale):

    def single_head(items):
        query_one, grad_one, key_one, value_one = items
        scores = (
            jnp.einsum("id,jd->ij", query_one, key_one, preferred_element_type=jnp.float32)
            * score_scale
        )
        scores = jnp.where(allowed, scores, masked_score)
        top_score = jnp.max(scores, axis=1, keepdims=True)
        log_total = top_score + jnp.log(jnp.sum(jnp.exp(scores - top_score), axis=1, keepdims=True))
        prob_float = jnp.where(allowed, jnp.exp(scores - log_total), 0.0)
        prob_half = prob_float.astype(jnp.bfloat16)
        out_float = jnp.einsum(
            "ij,jd->id", prob_half, value_one, preferred_element_type=jnp.float32
        )
        correction = jnp.sum(grad_one.astype(jnp.float32) * out_float, axis=1)
        grad_prob = jnp.einsum("id,jd->ij", grad_one, value_one, preferred_element_type=jnp.float32)
        grad_score = (prob_float * (grad_prob - correction[:, None]) * score_scale).astype(
            jnp.bfloat16
        )
        query_part = jnp.einsum(
            "ij,jd->id", grad_score, key_one, preferred_element_type=jnp.float32
        ).astype(jnp.bfloat16)
        key_part = jnp.einsum(
            "ij,id->jd", grad_score, query_one, preferred_element_type=jnp.float32
        )
        value_part = jnp.einsum(
            "ij,id->jd", prob_half, grad_one, preferred_element_type=jnp.float32
        )
        return (out_float.astype(jnp.bfloat16), query_part, key_part, value_part)

    items = tuple(
        (jnp.moveaxis(array, 1, 0) for array in (query_block, grad_block, key_window, value_window))
    )
    results = lax.map(single_head, items)
    return tuple((jnp.moveaxis(array, 0, 1) for array in results))


def per_device(query_rows, key_rows, value_rows, out_grad, clip_lengths):
    query_local, key_local, value_local, grad_local = (
        lax.all_to_all(query_rows, "tp", split_axis=1, concat_axis=0, tiled=True),
        lax.all_to_all(key_rows, "tp", split_axis=1, concat_axis=0, tiled=True),
        lax.all_to_all(value_rows, "tp", split_axis=1, concat_axis=0, tiled=True),
        lax.all_to_all(out_grad, "tp", split_axis=1, concat_axis=0, tiled=True),
    )
    row_count, feature_count = query_local.shape
    head_count = feature_count // DH
    score_scale = DH ** (-0.5)
    shard_index = lax.axis_index(("enc", "ctx"))
    seq_total = row_count * lax.axis_size(("enc", "ctx"))
    positions = shard_index * row_count + jnp.arange(-row_count, 2 * row_count, dtype=jnp.int32)
    clip_ids = clip_numbers(positions, clip_lengths)
    inside = (positions >= 0) & (positions < seq_total)
    query_heads = query_local.reshape(row_count, head_count, DH)
    grad_heads = grad_local.reshape(row_count, head_count, DH)
    key_value = padded(jnp.stack((key_local, value_local)), ((("enc", "ctx"), 1),), row_count)
    key_window = key_value[0].reshape(3 * row_count, head_count, DH)
    value_window = key_value[1].reshape(3 * row_count, head_count, DH)
    own_ids = clip_ids[row_count : 2 * row_count]
    allowed = (own_ids[:, None] == clip_ids[None, :]) & inside[None, :]
    out_part, query_part, key_terms, value_terms = window_pass(
        query_heads, grad_heads, key_window, value_window, allowed, score_scale
    )
    lower_terms = jnp.stack((key_terms[:row_count], value_terms[:row_count]))
    upper_terms = jnp.stack((key_terms[2 * row_count :], value_terms[2 * row_count :]))
    from_above = from_behind(lower_terms, ("enc", "ctx"), -1)
    from_below = from_behind(upper_terms, ("enc", "ctx"), 1)
    key_total = key_terms[row_count : 2 * row_count] + from_above[0] + from_below[0]
    value_total = value_terms[row_count : 2 * row_count] + from_above[1] + from_below[1]
    attended_heads = out_part.reshape(row_count, feature_count)
    query_heads_grad = query_part.reshape(row_count, feature_count)
    key_heads_grad = key_total.astype(jnp.bfloat16).reshape(row_count, feature_count)
    value_heads_grad = value_total.astype(jnp.bfloat16).reshape(row_count, feature_count)
    attended, query_grad, key_grad, value_grad = (
        lax.all_to_all(attended_heads, "tp", split_axis=0, concat_axis=1, tiled=True),
        lax.all_to_all(query_heads_grad, "tp", split_axis=0, concat_axis=1, tiled=True),
        lax.all_to_all(key_heads_grad, "tp", split_axis=0, concat_axis=1, tiled=True),
        lax.all_to_all(value_heads_grad, "tp", split_axis=0, concat_axis=1, tiled=True),
    )
    return (attended, query_grad, key_grad, value_grad)


def solution(mesh):
    in_specs = (
        P(("enc", "ctx", "tp"), None),
        P(("enc", "ctx", "tp"), None),
        P(("enc", "ctx", "tp"), None),
        P(("enc", "ctx", "tp"), None),
        P(),
    )
    out_specs = (
        P(("enc", "ctx", "tp"), None),
        P(("enc", "ctx", "tp"), None),
        P(("enc", "ctx", "tp"), None),
        P(("enc", "ctx", "tp"), None),
    )
    return jax.shard_map(
        per_device, mesh=mesh, in_specs=in_specs, out_specs=out_specs, check_vma=False
    )
```

profile of v0, /device:TPU:8, one launch (start us, length us, event | category | flops | bytes accessed | tf_op | source)
XLA Modules:
  0.0 1098.5 jit_solution(11788748281163539820)
XLA Ops:
  10.8 25.2 %all-to-all-done.1 = bf16[192,4,1536]{2,0,1:T(8,128)(2,1)S(1)} async-done(((bf16[192,4,1536]{2,0,1:T(8,128)(2,1)}), bf16[192,4,1536]{2,0,1:T(8,128)(2,1)S(1)}, u32[]{:S(2)}, u32[]{:S(2)}) %all-to-all-start.1) | async-done | bytes 2359328 | tf_op jit(solution)/shard_map/all_to_all | solution.py:82
  36.0 32.1 %all_to_all.140 = bf16[192,4,1536]{2,0,1:T(8,128)(2,1)S(1)} all-to-all(bf16[192,4,1536]{2,0,1:T(8,128)(2,1)} %bitcast.180), channel_id=1, replica_groups=mesh['enc'=2,'ctx'=4,'tp'=4] {'tp'}, dimensions={1} | all-to-all | bytes 4718592 | tf_op jit(solution)/shard_map/all_to_all | solution.py:83
  78.7 4.5 all-to-all-start
  86.5 25.3 %all-to-all-done = bf16[192,4,1536]{2,0,1:T(8,128)(2,1)} async-done(((bf16[192,4,1536]{2,0,1:T(8,128)(2,1)}), bf16[192,4,1536]{2,0,1:T(8,128)(2,1)}, u32[]{:S(2)}, u32[]{:S(2)}) %all-to-all-start) | async-done | bytes 2359328 | tf_op jit(solution)/shard_map/all_to_all | solution.py:81
  111.8 4.5 all-to-all-start.3
  116.7 5.4 reshape.99
  126.0 18.8 %all-to-all-done.3 = bf16[192,4,1536]{2,0,1:T(8,128)(2,1)} async-done(((bf16[192,4,1536]{2,0,1:T(8,128)(2,1)}), bf16[192,4,1536]{2,0,1:T(8,128)(2,1)}, u32[]{:S(2)}, u32[]{:S(2)}) %all-to-all-start.3) | async-done | bytes 2359328 | tf_op jit(solution)/shard_map/all_to_all | solution.py:84
  144.8 5.4 reshape.102
  150.2 4.8 copy.78
  155.1 22.1 %collective-permute-done.1 = bf16[2,768,1536]{2,1,0:T(8,128)(2,1)} collective-permute-done((bf16[2,768,1536]{2,1,0:T(8,128)(2,1)}, bf16[2,768,1536]{2,1,0:T(8,128)(2,1)}, u32[]{:S(2)}, u32[]{:S(2)}) %collective-permute-start.1) | collective-permute-done | bytes 4718624 | tf_op jit(solution)/shard_map/ppermute | solution.py:22
  178.6 6.1 pad_maximum_fusion
  184.7 5.2 fusion.37
  189.9 10.2 copy.71
  200.1 10.5 copy.70
  210.7 280.7 %while.17 = (s32[]{:T(128)}, bf16[12,768,128]{1,2,0:T(8,128)(2,1)S(1)}, bf16[12,768,128]{2,1,0:T(8,128)(2,1)}, f32[12,2304,128]{2,1,0:T(8,128)}, f32[12,2304,128...) while((s32[]{:T(128)}, ...), condition=%wide.region_6.7_spmd.clone, body=%wide.region_2.6_spmd.clone.sunk | while | flops 2753788416 | bytes 56507272 | solution.py:75
  220.8 4.2 multiply_convert_fusion.2
  267.6 4.2 multiply_convert_fusion.2
  431.4 4.2 multiply_convert_fusion.2
  492.8 8.1 slice_bitcast_fusion.6
  500.9 4.2 pad_maximum_fusion.2
  508.7 4.2 pad_maximum_fusion.1
  512.9 5.8 collective-permute-start.2
  518.8 6.1 reshape.103
  528.4 4.5 all-to-all-start.4
  539.1 22.4 %all-to-all-done.4 = bf16[4,192,1536]{2,1,0:T(8,128)(2,1)} async-done(((bf16[4,192,1536]{2,1,0:T(8,128)(2,1)}), bf16[4,192,1536]{2,1,0:T(8,128)(2,1)}, u32[]{:S(2)}, u32[]{:S(2)}) %all-to-all-start.4) | async-done | bytes 2359328 | tf_op jit(solution)/shard_map/all_to_all | solution.py:115
  561.5 4.5 all-to-all-start.5
  566.0 144.7 %collective-permute-done.3 = f32[2,768,12,128]{3,1,2,0:T(8,128)} collective-permute-done((f32[2,768,12,128]{3,1,2,0:T(8,128)}, f32[2,768,12,128]{3,1,2,0:T(8,128)}, u32[]{:S(2)}, u32[]{:S(2)}) %collective-permute-start.3) | collective-permute-done | bytes 9437216 | tf_op jit(solution)/shard_map/ppermute | solution.py:32
  710.7 305.2 %collective-permute-done.2 = f32[2,768,12,128]{3,1,2,0:T(8,128)} collective-permute-done((f32[2,768,12,128]{3,1,2,0:T(8,128)}, f32[2,768,12,128]{3,1,2,0:T(8,128)}, u32[]{:S(2)}, u32[]{:S(2)}) %collective-permute-start.2) | collective-permute-done | bytes 9437216 | tf_op jit(solution)/shard_map/ppermute | solution.py:32
  1015.9 11.3 %fusion.31 = (bf16[768,12,128]{2,0,1:T(8,128)(2,1)S(1)}, bf16[768,12,128]{2,0,1:T(8,128)(2,1)}) fusion(f32[2,768,12,128]{3,1,2,0:T(8,128)} %collective-permute-done.3, f32[2,768,12,128]{3,1,2,0:T(8,128)} %collective-permute-done.2, f32[2304,12,128]{2,0,1:T(8,128)} %bitcast.172, f32[2304,12,128]{2,0,1:T(8,128)} %bitcast.174), kind=kLoop, calls=%fused_computation.45 | loop fusion | flops 7077888 | bytes 33030144 | tf_op jit(solution)/shard_map/convert_element_type | solution.py:113
  1031.7 4.5 all-to-all-start.7
  1042.3 22.4 %all-to-all-done.7 = bf16[4,192,1536]{2,1,0:T(8,128)(2,1)} async-done(((bf16[4,192,1536]{2,1,0:T(8,128)(2,1)}), bf16[4,192,1536]{2,1,0:T(8,128)(2,1)}, u32[]{:S(2)}, u32[]{:S(2)}) %all-to-all-start.7) | async-done | bytes 2359328 | tf_op jit(solution)/shard_map/all_to_all | solution.py:118
  1078.4 18.3 %all-to-all-done.6 = bf16[4,192,1536]{2,1,0:T(8,128)(2,1)S(1)} async-done(((bf16[4,192,1536]{2,1,0:T(8,128)(2,1)}), bf16[4,192,1536]{2,1,0:T(8,128)(2,1)S(1)}, u32[]{:S(2)}, u32[]{:S(2)}) %all-to-all-start.6) | async-done | bytes 2359328 | tf_op jit(solution)/shard_map/all_to_all | solution.py:117
  (162 shorter events, 338.4 us)
Async XLA Ops:
  3.9 32.1 %all-to-all-start.1 = ((bf16[192,4,1536]{2,0,1:T(8,128)(2,1)}), bf16[192,4,1536]{2,0,1:T(8,128)(2,1)S(1)}, u32[]{:S(2)}, u32[]{:S(2)}) async-start(bf16[192,4,1536]{2,0,1:T(8,128)(2,1)} %bitcast.179), calls=%async_computation.1 | async-start | bytes 4718592 | tf_op jit(solution)/shard_map/all_to_all | solution.py:82
  68.1 3.2 copy-start
  68.1 9.0 copy-start.1
  71.3 105.9 %collective-permute-start.1 = (bf16[2,768,1536]{2,1,0:T(8,128)(2,1)}, bf16[2,768,1536]{2,1,0:T(8,128)(2,1)}, u32[]{:S(2)}, u32[]{:S(2)}) collective-permute-start(bf16[2,768,1536]{2,1,0:T(8,128)(2,1)} %pad_maximum_fusion.3), channel_id=1, source_target_pairs={{4,0},{8,4},{12,8},{16,12},{20,16},{24,20},{28,24},{5,1},{9,5},{13... | collective-permute-start | bytes 14155784 | tf_op jit(solution)/shard_map/ppermute | solution.py:22
  73.2 105.4 %collective-permute-start = (bf16[2,768,1536]{2,1,0:T(8,128)(2,1)}, bf16[2,768,1536]{2,1,0:T(8,128)(2,1)}, u32[]{:S(2)}, u32[]{:S(2)}) collective-permute-start(bf16[2,768,1536]{2,1,0:T(8,128)(2,1)} %pad_maximum_fusion.3), channel_id=1, source_target_pairs={{0,4},{4,8},{8,12},{12,16},{16,20},{20,24},{24,28},{1,5},{5,9},{9,... | collective-permute-start | bytes 14155784 | tf_op jit(solution)/shard_map/ppermute | solution.py:20
  78.7 33.1 %all-to-all-start = ((bf16[192,4,1536]{2,0,1:T(8,128)(2,1)}), bf16[192,4,1536]{2,0,1:T(8,128)(2,1)}, u32[]{:S(2)}, u32[]{:S(2)}) async-start(bf16[192,4,1536]{2,0,1:T(8,128)(2,1)} %bitcast.181), calls=%async_computation | async-start | bytes 4718592 | tf_op jit(solution)/shard_map/all_to_all | solution.py:81
  83.2 33.1 %copy-start.4 = (s32[16]{0:T(128)S(1)}, s32[16]{0:T(128)}, u32[]{:S(2)}) copy-start(s32[16]{0:T(128)} %param.11) | copy-start | bytes 196
  111.8 33.0 %all-to-all-start.3 = ((bf16[192,4,1536]{2,0,1:T(8,128)(2,1)}), bf16[192,4,1536]{2,0,1:T(8,128)(2,1)}, u32[]{:S(2)}, u32[]{:S(2)}) async-start(bf16[192,4,1536]{2,0,1:T(8,128)(2,1)} %bitcast.177), calls=%async_computation.3 | async-start | bytes 4718592 | tf_op jit(solution)/shard_map/all_to_all | solution.py:84
  200.1 10.5 copy-start.2
  491.4 1.4 copy-start.3
  505.1 205.6 %collective-permute-start.3 = (f32[2,768,12,128]{3,1,2,0:T(8,128)}, f32[2,768,12,128]{3,1,2,0:T(8,128)}, u32[]{:S(2)}, u32[]{:S(2)}) collective-permute-start(f32[2,768,12,128]{3,1,2,0:T(8,128)} %pad_maximum_fusion.2), channel_id=1, source_target_pairs={{0,4},{4,8},{8,12},{12,16},{16,20},{20,24},{24,28},{1,5},{5,9},{9,... | collective-permute-start | bytes 28311560 | tf_op jit(solution)/shard_map/ppermute | solution.py:32
  512.9 503.0 %collective-permute-start.2 = (f32[2,768,12,128]{3,1,2,0:T(8,128)}, f32[2,768,12,128]{3,1,2,0:T(8,128)}, u32[]{:S(2)}, u32[]{:S(2)}) collective-permute-start(f32[2,768,12,128]{3,1,2,0:T(8,128)} %pad_maximum_fusion.1), channel_id=1, source_target_pairs={{4,0},{8,4},{12,8},{16,12},{20,16},{24,20},{28,24},{5,1},{9,5},{13... | collective-permute-start | bytes 28311560 | tf_op jit(solution)/shard_map/ppermute | solution.py:32
  528.4 33.1 %all-to-all-start.4 = ((bf16[4,192,1536]{2,1,0:T(8,128)(2,1)}), bf16[4,192,1536]{2,1,0:T(8,128)(2,1)}, u32[]{:S(2)}, u32[]{:S(2)}) async-start(bf16[4,192,1536]{2,1,0:T(8,128)(2,1)} %copy.87), calls=%async_computation.4 | async-start | bytes 4718592 | tf_op jit(solution)/shard_map/all_to_all | solution.py:115
  561.5 470.2 %all-to-all-start.5 = ((bf16[4,192,1536]{2,1,0:T(8,128)(2,1)}), bf16[4,192,1536]{2,1,0:T(8,128)(2,1)}, u32[]{:S(2)}, u32[]{:S(2)}) async-start(bf16[4,192,1536]{2,1,0:T(8,128)(2,1)} %all_to_all.120), calls=%async_computation.5 | async-start | bytes 4718592 | tf_op jit(solution)/shard_map/all_to_all | solution.py:116
  1031.7 33.0 %all-to-all-start.7 = ((bf16[4,192,1536]{2,1,0:T(8,128)(2,1)}), bf16[4,192,1536]{2,1,0:T(8,128)(2,1)}, u32[]{:S(2)}, u32[]{:S(2)}) async-start(bf16[4,192,1536]{2,1,0:T(8,128)(2,1)} %all_to_all.128), calls=%async_computation.7 | async-start | bytes 4718592 | tf_op jit(solution)/shard_map/all_to_all | solution.py:118
  1064.7 32.1 %all-to-all-start.6 = ((bf16[4,192,1536]{2,1,0:T(8,128)(2,1)}), bf16[4,192,1536]{2,1,0:T(8,128)(2,1)S(1)}, u32[]{:S(2)}, u32[]{:S(2)}) async-start(bf16[4,192,1536]{2,1,0:T(8,128)(2,1)} %all_to_all.124), calls=%async_computation.6 | async-start | bytes 4718592 | tf_op jit(solution)/shard_map/all_to_all | solution.py:117
where the time goes:
time: 1100 us
  waiting for transfers between devices  606 us (55%)
  matrix products  224 us (20%)
  local copies, waits for them, and re-layouts  105 us (10%)
  other arithmetic  84.7 us (8%)
  starting transfers between devices  45.1 us (4%)
  blocking collectives  32.1 us (3%)
    ppermute x2, waiting for transfers between devices, from_behind(): return lax.ppermute(block, axis, route)  450 us
    dot_general x12, matrix products, single_head(): jnp.einsum('id,jd->ij', grad_one, value_one, preferred_element_type=jnp.f...  50 us
    dot_general x12, matrix products, single_head(): jnp.einsum('id,jd->ij', query_one, key_one, preferred_element_type=jnp.fl...  37.8 us
    dot_general x12, matrix products, single_head(): jnp.einsum('ij,id->jd', grad_score, query_one, preferred_element_type=jnp...  37.3 us
    dot_general x12, matrix products, single_head(): jnp.einsum('ij,id->jd', prob_half, grad_one, preferred_element_type=jnp.f...  37.2 us
    dot_general x12, matrix products, single_head(): jnp.einsum('ij,jd->id', grad_score, key_one, preferred_element_type=jnp.f...  33.9 us
    all_to_all x1, blocking collectives, per_device(): lax.all_to_all(value_rows, 'tp', split_axis=1, concat_axis=0, tiled=True)  32.1 us
    convert_element_type x12, other arithmetic, single_head(): prob_half = prob_float.astype(jnp.bfloat16)  30.6 us
  transfers between devices with their start and end apart: 11, of which 10 were waited for; matrix products, arithmetic and copies ran while one was open for 7% of the time, Pallas kernels for 0%

commit v1 on v0

v1 whole, which is shorter than its diff:
```python
import functools
import math

import jax
import jax.numpy as jnp
from jax import lax
from jax.experimental import pallas as pl
from jax.experimental.pallas import tpu as pltpu
from jax.sharding import PartitionSpec as P

DH = 128
GROUPS = 3
TILE = 256
ALIGN = 128
MASKED = -1e30


def widths(window):
    steps = sorted({min(w, window) for w in (256, 512, 768, 1024, window)})
    return tuple(steps)


def attention_kernel(
    plan_ref, low_ref, own_ref, high_ref, row_ids, key_ids,
    low_out, own_out, high_out,
    q_win, k_win, v_win, g_win, out_win, dq_win, dk_win, dv_win,
):
    block = pl.program_id(0)
    rows = own_ref.shape[3]
    pieces = [(low_ref, t) for t in range(low_ref.shape[1])]
    pieces += [(own_ref, t) for t in range(own_ref.shape[1])]
    pieces += [(high_ref, t) for t in range(high_ref.shape[1])]
    window = q_win.shape[0]
    for n, (ref, t) in enumerate(pieces):
        for a, win in enumerate((q_win, k_win, v_win, g_win)):
            win[pl.ds(n * rows, rows), :] = ref[0, t, a]
    dk_win[...] = jnp.zeros_like(dk_win)
    dv_win[...] = jnp.zeros_like(dv_win)
    tiles = window // TILE
    scale = DH ** -0.5
    log_scale = scale * math.log2(math.e)

    def work(i, start, width):
        here = pl.ds(pl.multiple_of(i * TILE, TILE), TILE)
        keys = pl.ds(pl.multiple_of(start, ALIGN), width)
        q, g = q_win[here, :], g_win[here, :]
        k, v = k_win[keys, :], v_win[keys, :]
        allowed = row_ids[0, here, :] == key_ids[0, :, keys]
        across = (((1,), (1,)), ((), ()))
        down = (((0,), (0,)), ((), ()))
        s = lax.dot_general(q, k, across, preferred_element_type=jnp.float32)
        s = jnp.where(allowed, s * log_scale, MASKED)
        top = jnp.maximum(jnp.max(s, axis=1, keepdims=True), 0.1 * MASKED)
        e = jnp.exp2(s - top)
        total = jnp.sum(e, axis=1, keepdims=True)
        p = e * (1.0 / jnp.where(total > 0.0, total, 1.0))
        half = p.astype(jnp.bfloat16)
        out = jnp.dot(half, v, preferred_element_type=jnp.float32)
        correction = jnp.sum(g.astype(jnp.float32) * out, axis=1, keepdims=True)
        gp = lax.dot_general(g, v, across, preferred_element_type=jnp.float32)
        ds = (p * (gp - correction)).astype(jnp.bfloat16)
        dq = jnp.dot(ds, k, preferred_element_type=jnp.float32) * scale
        out_win[here, :] = out.astype(jnp.bfloat16)
        dq_win[here, :] = dq.astype(jnp.bfloat16)
        dk_win[keys, :] += lax.dot_general(ds, q, down, preferred_element_type=jnp.float32)
        dv_win[keys, :] += lax.dot_general(half, g, down, preferred_element_type=jnp.float32)

    def one_tile(i, carry):
        start = plan_ref[block, 0, i]
        kind = plan_ref[block, 1, i]
        for n, width in enumerate(widths(window)):
            pl.when(kind == n + 1)(functools.partial(work, i, start, width))
        return carry

    lax.fori_loop(0, tiles, one_tile, 0)
    targets = [(low_out, t) for t in range(low_ref.shape[1])]
    targets += [(own_out, t) for t in range(own_ref.shape[1])]
    targets += [(high_out, t) for t in range(high_ref.shape[1])]
    for n, (ref, t) in enumerate(targets):
        part = pl.ds(n * rows, rows)
        ref[0, t, 0] = out_win[part, :]
        ref[0, t, 1] = dq_win[part, :]
        ref[0, t, 2] = (dk_win[part, :] * scale).astype(jnp.bfloat16)
        ref[0, t, 3] = dv_win[part, :].astype(jnp.bfloat16)


def attention(plan, low, own, high, row_ids, key_ids):
    blocks, parts, arrays, rows, features = own.shape
    side = low.shape[1]
    window = (parts + 2 * side) * rows
    heads = features // DH

    def spec(count):
        return pl.BlockSpec((1, count, arrays, rows, DH), lambda e, h, plan: (e, 0, 0, 0, h))

    grid_spec = pltpu.PrefetchScalarGridSpec(
        num_scalar_prefetch=1,
        grid=(blocks, heads),
        in_specs=[
            spec(side),
            spec(parts),
            spec(side),
            pl.BlockSpec((1, window, 1), lambda e, h, plan: (e, 0, 0)),
            pl.BlockSpec((1, 1, window), lambda e, h, plan: (e, 0, 0)),
        ],
        out_specs=[spec(side), spec(parts), spec(side)],
        scratch_shapes=[pltpu.VMEM((window, DH), jnp.bfloat16)] * 6
        + [pltpu.VMEM((window, DH), jnp.float32)] * 2,
    )
    pairs = blocks * heads * window * 768
    return pl.pallas_call(
        attention_kernel,
        grid_spec=grid_spec,
        out_shape=[jax.ShapeDtypeStruct(x.shape, x.dtype) for x in (low, own, high)],
        compiler_params=pltpu.CompilerParams(vmem_limit_bytes=48 * 1024 * 1024),
        cost_estimate=pl.CostEstimate(
            flops=10 * pairs * DH,
            bytes_accessed=4 * (own.size + 2 * low.size),
            transcendentals=pairs,
        ),
    )(plan, low, own, high, row_ids, key_ids)


def from_previous(x):
    count = lax.axis_size("ctx")
    got = lax.ppermute(x, "ctx", [(i, i + 1) for i in range(count - 1)])
    wrapped = lax.ppermute(x[:-1], "ctx", [(count - 1, 0)])
    wrapped = jnp.concatenate([jnp.zeros_like(x[:1]), wrapped], axis=0)
    return jnp.where(lax.axis_index("ctx") == 0, wrapped, got)


def from_next(x):
    count = lax.axis_size("ctx")
    got = lax.ppermute(x, "ctx", [(i + 1, i) for i in range(count - 1)])
    wrapped = lax.ppermute(x[1:], "ctx", [(0, count - 1)])
    wrapped = jnp.concatenate([wrapped, jnp.zeros_like(x[:1])], axis=0)
    return jnp.where(lax.axis_index("ctx") == count - 1, wrapped, got)


def clip_plan(clip_lengths, block_rows, side_rows, enc, ctx):
    length = block_rows * enc * ctx
    window = block_rows + 2 * side_rows
    ends = jnp.cumsum(clip_lengths).astype(jnp.int32)
    starts = ends - clip_lengths
    first, last = starts // block_rows, (ends - 1) // block_rows
    edge = last * block_rows
    owner = jnp.where((first == last) | (edge - starts >= ends - edge), first, last)

    block = jnp.arange(enc, dtype=jnp.int32) * ctx + lax.axis_index("ctx")
    base = block * block_rows - side_rows
    position = base[:, None] + jnp.arange(window, dtype=jnp.int32)[None]
    inside = (position >= starts[:, None, None]) & (position < ends[:, None, None])

    def look(table):
        return jnp.sum(jnp.where(inside, table[:, None, None], 0), axis=0)

    numbers = look(jnp.arange(1, clip_lengths.shape[0] + 1, dtype=jnp.int32))
    owners = look(owner + 1) - 1
    mine = owners == block[:, None]
    row_ids = jnp.where(mine, numbers, -1)
    key_ids = jnp.where(mine, numbers, -2)
    low = jnp.where(mine, look(starts) - base[:, None], window).reshape(enc, -1, TILE).min(axis=2)
    top = jnp.where(mine, look(ends) - base[:, None], 0).reshape(enc, -1, TILE).max(axis=2)
    low = (low // ALIGN) * ALIGN
    need = top - low
    sizes = widths(window)
    kind = jnp.ones_like(need)
    chosen = jnp.full_like(need, sizes[0])
    for n in range(1, len(sizes)):
        more = need > sizes[n - 1]
        kind = jnp.where(more, n + 1, kind)
        chosen = jnp.where(more, sizes[n], chosen)
    kind = jnp.where(need > 0, kind, 0)
    low = jnp.clip(low, 0, window - chosen)
    plan = jnp.stack([low, kind], axis=1).astype(jnp.int32)
    own = owners[:, side_rows : side_rows + block_rows]
    before = own < block[:, None]
    after = own > block[:, None]
    return plan, row_ids[:, :, None], key_ids[:, None, :], before, after


def per_device(query_rows, key_rows, value_rows, out_grad, clip_lengths):
    enc, ctx, tp = (lax.axis_size(a) for a in ("enc", "ctx", "tp"))
    team = enc * tp
    rows, features = query_rows.shape
    wide = features // (team * GROUPS)
    side = tp // 2
    plan, row_ids, key_ids, before, after = clip_plan(
        clip_lengths, rows * tp, rows * side, enc, ctx
    )
    before = before.reshape(enc, tp, 1, rows, 1)[:, :side]
    after = after.reshape(enc, tp, 1, rows, 1)[:, tp - side :]
    arrays = [
        a.reshape(rows, team, GROUPS, wide) for a in (query_rows, key_rows, value_rows, out_grad)
    ]
    axes = ("enc", "tp")
    results = []
    for g in range(GROUPS):
        sent = jnp.stack([a[:, :, g].transpose(1, 0, 2) for a in arrays], axis=1)
        own = lax.all_to_all(sent, axes, split_axis=0, concat_axis=0, tiled=True)
        own = own.reshape(enc, tp, 4, rows, wide)
        low = from_previous(own[:, tp - side :])
        high = from_next(own[:, :side])
        low_out, own_out, high_out = attention(plan, low, own, high, row_ids, key_ids)
        back_low = from_previous(high_out)
        back_high = from_next(low_out)
        total = jnp.concatenate(
            [
                jnp.where(before, back_low, own_out[:, :side]),
                jnp.where(after, back_high, own_out[:, tp - side :]),
            ],
            axis=1,
        ).reshape(team, 4, rows, wide)
        results.append(lax.all_to_all(total, axes, split_axis=0, concat_axis=0, tiled=True))
    done = []
    for a in range(4):
        joined = jnp.stack([r[:, a] for r in results], axis=1)
        done.append(joined.transpose(2, 0, 1, 3).reshape(rows, features))
    return tuple(done)


def solution(mesh):
    spec = P(("enc", "ctx", "tp"), None)
    return jax.shard_map(
        per_device,
        mesh=mesh,
        in_specs=(spec, spec, spec, spec, P()),
        out_specs=(spec, spec, spec, spec),
        check_vma=False,
    )
```

time: 1100 us -> 692 us (0.63)
  the two profiles are of different devices: /device:TPU:8 before, /device:TPU:0 now
where the time goes in v1:
time: 692 us; the launch traced here: 686 us
  waiting for transfers between devices  289 us (42%)
  local copies, waits for them, and re-layouts  154 us (22%)
  starting transfers between devices  126 us (18%)
  Pallas kernels  66.9 us (10%)
  other arithmetic  48.5 us (7%)
    ppermute x6, waiting for transfers between devices, from_previous(): wrapped = lax.ppermute(x[:-1], 'ctx', [(count - 1, 0)])  112 us
    all_to_all x3, waiting for transfers between devices, per_device(): own = lax.all_to_all(sent, axes, split_axis=0, concat_axis=0, tiled=True)  74.5 us
    pallas_call x3, Pallas kernels, attention(): pl.pallas_call(attention_kernel, grid_spec=grid_spec, out_shape=[jax.Shap...  66.9 us
    ppermute x6, starting transfers between devices, from_next(): wrapped = lax.ppermute(x[1:], 'ctx', [(0, count - 1)])  57.2 us
    ppermute x6, waiting for transfers between devices, from_next(): wrapped = lax.ppermute(x[1:], 'ctx', [(0, count - 1)])  50.3 us
    all_to_all x3, waiting for transfers between devices, per_device(): lax.all_to_all(total, axes, split_axis=0, concat_axis=0, tiled=True)  49.9 us
    slice x3, local copies, waits for them, and re-layouts, per_device(): joined = jnp.stack([r[:, a] for r in results], axis=1)  30.6 us
    ppermute x6, starting transfers between devices, from_previous(): got = lax.ppermute(x, 'ctx', [(i, i + 1) for i in range(count - 1)])  27.2 us
  transfers between devices with their start and end apart: 30, of which 10 were waited for; matrix products, arithmetic and copies ran while one was open for 10% of the time, Pallas kernels for 10%

profile of v1, /device:TPU:0, one launch (start us, length us, event | category | flops | bytes accessed | tf_op | source)
XLA Modules:
  0.0 686.3 jit_solution(10342099307806280327)
XLA Ops:
  0.6 6.1 reshape.342
  11.7 6.1 reshape.341
  22.7 6.1 reshape.340
  28.8 5.0 fusion.11
  33.7 6.1 reshape.339
  53.5 5.2 all-to-all-start.4
  65.2 31.4 %all-to-all-done.4 = bf16[8,4,192,256]{3,2,1,0:T(8,128)(2,1)S(1)} async-done(((bf16[8,4,192,256]{3,2,1,0:T(8,128)(2,1)}), bf16[8,4,192,256]{3,2,1,0:T(8,128)(2,1)S(1)}, u32[]{:S(2)}, u32[]{:S(2)}) %all-to-all-start.4) | async-done | bytes 3145760 | tf_op jit(solution)/shard_map/all_to_all | solution.py:200
  107.2 32.8 %all-to-all-done = bf16[8,4,192,256]{3,2,1,0:T(8,128)(2,1)S(1)} async-done(((bf16[8,4,192,256]{3,2,1,0:T(8,128)(2,1)}), bf16[8,4,192,256]{3,2,1,0:T(8,128)(2,1)S(1)}, u32[]{:S(2)}, u32[]{:S(2)}) %all-to-all-start) | async-done | bytes 3145760 | tf_op jit(solution)/shard_map/all_to_all | solution.py:200
  160.6 5.7 collective-permute-start.1
  172.8 10.3 %all-to-all-done.2 = bf16[8,4,192,256]{3,2,1,0:T(8,128)(2,1)S(1)} async-done(((bf16[8,4,192,256]{3,2,1,0:T(8,128)(2,1)}), bf16[8,4,192,256]{3,2,1,0:T(8,128)(2,1)S(1)}, u32[]{:S(2)}, u32[]{:S(2)}) %all-to-all-start.2) | async-done | bytes 3145760 | tf_op jit(solution)/shard_map/all_to_all | solution.py:200
  192.3 46.1 %collective-permute-done.18 = bf16[1,2,4,192,256]{4,3,2,1,0:T(8,128)(2,1)} collective-permute-done((bf16[1,2,4,192,256]{4,3,2,1,0:T(8,128)(2,1)}, bf16[1,2,4,192,256]{4,3,2,1,0:T(8,128)(2,1)}, u32[]{:S(2)}, u32[]{:S(2)}) %collective-permute-start.18) | collective-permute-done | bytes 786464 | tf_op jit(solution)/shard_map/ppermute | solution.py:135
  238.4 6.3 collective-permute-start.2
  251.6 22.3 %shard_map.86 = (bf16[2,2,4,192,256]{4,3,2,1,0:T(8,128)(2,1)S(1)}, bf16[2,4,4,192,256]{4,3,2,1,0:T(8,128)(2,1)}, bf16[2,2,4,192,256]{4,3,2,1,0:T(8,128)(2,1)}) custom-call(s32[2,2,6]{2,1,0:T(2,128)S(1)} %pad_add_fusion.plan_ref, bf16[2,2,4,192,256]{4,3,2,1,0:T(8,128)(2,1)S(1)} %pad_select_fusion.1.low_ref, bf16[2,4,4,192,256]{4,3,2,1,0:T(8,128)(2,1)} %bitcast.110, ...), custom_call_target="tpu_custom_call" | custom-call | flops 6039797760 | bytes 12582912 | tf_op jit(solution)/shard_map/pallas_call | solution.py:111
  277.2 19.6 %collective-permute-start.10 = (bf16[1,2,4,192,256]{4,3,2,1,0:T(8,128)(2,1)}, bf16[1,2,4,192,256]{4,3,2,1,0:T(8,128)(2,1)}, u32[]{:S(2)}, u32[]{:S(2)}) collective-permute-start(bf16[1,2,4,192,256]{4,3,2,1,0:T(8,128)(2,1)} %get-tuple-element.64), channel_id=1, source_target_pairs={{0,12},{1,13},{2,14},{3,15},{16,28},{17,29},{18,30},{19,31}} | collective-permute-start | bytes 2359304 | tf_op jit(solution)/shard_map/ppermute | solution.py:135
  298.1 6.8 collective-permute-start.22
  307.3 22.2 %shard_map.84 = (bf16[2,2,4,192,256]{4,3,2,1,0:T(8,128)(2,1)}, bf16[2,4,4,192,256]{4,3,2,1,0:T(8,128)(2,1)}, bf16[2,2,4,192,256]{4,3,2,1,0:T(8,128)(2,1)}) custom-call(s32[2,2,6]{2,1,0:T(2,128)S(1)} %pad_add_fusion.plan_ref, bf16[2,2,4,192,256]{4,3,2,1,0:T(8,128)(2,1)S(1)} %pad_select_fusion.5.low_ref, bf16[2,4,4,192,256]{4,3,2,1,0:T(8,128)(2,1)} %bitcast.106, ...), custom_call_target="tpu_custom_call" | custom-call | flops 6039797760 | bytes 12582912 | tf_op jit(solution)/shard_map/pallas_call | solution.py:111
  331.6 12.2 %collective-permute-start.6 = (bf16[1,2,4,192,256]{4,3,2,1,0:T(8,128)(2,1)}, bf16[1,2,4,192,256]{4,3,2,1,0:T(8,128)(2,1)}, u32[]{:S(2)}, u32[]{:S(2)}) collective-permute-start(bf16[1,2,4,192,256]{4,3,2,1,0:T(8,128)(2,1)} %slice.172), channel_id=1, source_target_pairs={{0,12},{1,13},{2,14},{3,15},{16,28},{17,29},{18,30},{19,31}} | collective-permute-start | bytes 2359304 | tf_op jit(solution)/shard_map/ppermute | solution.py:135
  348.9 6.3 collective-permute-start.5
  366.4 64.6 %collective-permute-done.4 = bf16[1,2,4,192,256]{4,3,2,1,0:T(8,128)(2,1)S(1)} collective-permute-done((bf16[1,2,4,192,256]{4,3,2,1,0:T(8,128)(2,1)S(1)}, bf16[1,2,4,192,256]{4,3,2,1,0:T(8,128)(2,1)S(1)}, u32[]{:S(2)}, u32[]{:S(2)}) %collective-permute-start.4) | collective-permute-done | bytes 786464 | tf_op jit(solution)/shard_map/ppermute | solution.py:127
  446.7 22.4 %shard_map.85 = (bf16[2,2,4,192,256]{4,3,2,1,0:T(8,128)(2,1)S(1)}, bf16[2,4,4,192,256]{4,3,2,1,0:T(8,128)(2,1)}, bf16[2,2,4,192,256]{4,3,2,1,0:T(8,128)(2,1)S(1)}) custom-call(s32[2,2,6]{2,1,0:T(2,128)S(1)} %pad_add_fusion.plan_ref, bf16[2,2,4,192,256]{4,3,2,1,0:T(8,128)(2,1)S(1)} %pad_select_fusion.3.low_ref, bf16[2,4,4,192,256]{4,3,2,1,0:T(8,128)(2,1)} %bitcast.105, ...), custom_call_target="tpu_custom_call" | custom-call | flops 6039797760 | bytes 12582912 | tf_op jit(solution)/shard_map/pallas_call | solution.py:111
  469.1 6.6 collective-permute-start.13
  478.7 7.5 %collective-permute-start.14 = (bf16[1,2,4,192,256]{4,3,2,1,0:T(8,128)(2,1)S(1)}, bf16[1,2,4,192,256]{4,3,2,1,0:T(8,128)(2,1)S(1)}, u32[]{:S(2)}, u32[]{:S(2)}) collective-permute-start(bf16[1,2,4,192,256]{4,3,2,1,0:T(8,128)(2,1)S(1)} %slice.185), channel_id=1, source_target_pairs={{0,12},{1,13},{2,14},{3,15},{16,28},{17,29},{18,30},{19,31}} | collective-permute-start | bytes 2359304 | tf_op jit(solution)/shard_map/ppermute | solution.py:135
  486.2 47.7 %collective-permute-done.12 = bf16[1,2,4,192,256]{4,3,2,1,0:T(8,128)(2,1)S(1)} collective-permute-done((bf16[1,2,4,192,256]{4,3,2,1,0:T(8,128)(2,1)S(1)}, bf16[1,2,4,192,256]{4,3,2,1,0:T(8,128)(2,1)S(1)}, u32[]{:S(2)}, u32[]{:S(2)}) %collective-permute-start.12) | collective-permute-done | bytes 786464 | tf_op jit(solution)/shard_map/ppermute | solution.py:127
  549.0 31.6 %all-to-all-done.3 = bf16[8,4,192,256]{3,1,2,0:T(4,128)(2,1)S(1)} async-done(((bf16[8,4,192,256]{3,1,2,0:T(4,128)(2,1)}), bf16[8,4,192,256]{3,1,2,0:T(4,128)(2,1)S(1)}, u32[]{:S(2)}, u32[]{:S(2)}) %all-to-all-start.3) | async-done | bytes 3145760 | tf_op jit(solution)/shard_map/all_to_all | solution.py:214
  585.3 11.5 %fusion.7 = (bf16[8,1,192,256]{3,1,2,0:T(2,128)(2,1)}, bf16[8,1,192,256]{3,1,2,0:T(2,128)(2,1)}, bf16[8,1,192,256]{3,1,2,0:T(2,128)(2,1)}, bf16[8,1,192,256]{3,1,2,0:T(2,128)(2,1)}) fusion(bf16[8,4,192,256]{3,1,2,0:T(4,128)(2,1)} %all-to-all-done.5), kind=kLoop, calls=%fused_computation.77 | loop fusion | bytes 6291456 | tf_op jit(solution)/shard_map/slice | solution.py:217
  596.8 8.0 %fusion.6 = (bf16[8,1,192,256]{3,1,2,0:T(2,128)(2,1)}, bf16[8,1,192,256]{3,1,2,0:T(2,128)(2,1)}, bf16[8,1,192,256]{3,1,2,0:T(2,128)(2,1)}, bf16[8,1,192,256]{3,1,2,0:T(2,128)(2,1)}) fusion(bf16[8,4,192,256]{3,1,2,0:T(4,128)(2,1)S(1)} %all-to-all-done.3), kind=kLoop, calls=%fused_computation.76 | loop fusion | bytes 6291456 | tf_op jit(solution)/shard_map/slice | solution.py:217
  604.8 18.4 %all-to-all-done.1 = bf16[8,4,192,256]{3,1,2,0:T(4,128)(2,1)} async-done(((bf16[8,4,192,256]{3,1,2,0:T(4,128)(2,1)}), bf16[8,4,192,256]{3,1,2,0:T(4,128)(2,1)}, u32[]{:S(2)}, u32[]{:S(2)}) %all-to-all-start.1) | async-done | bytes 3145760 | tf_op jit(solution)/shard_map/all_to_all | solution.py:214
  623.2 11.2 %fusion.5 = (bf16[8,1,192,256]{3,1,2,0:T(2,128)(2,1)}, bf16[8,1,192,256]{3,1,2,0:T(2,128)(2,1)}, bf16[8,1,192,256]{3,1,2,0:T(2,128)(2,1)}, bf16[8,1,192,256]{3,1,2,0:T(2,128)(2,1)S(1)}) fusion(bf16[8,4,192,256]{3,1,2,0:T(4,128)(2,1)} %all-to-all-done.1), kind=kLoop, calls=%fused_computation.75 | loop fusion | bytes 6291456 | tf_op jit(solution)/shard_map/slice | solution.py:217
  634.3 5.3 maximum_bitcast_fusion
  646.0 7.1 %maximum_bitcast_fusion.1 = bf16[192,8,3,256]{3,2,0,1:T(4,128)(2,1)S(1)} fusion(bf16[8,1,192,256]{3,1,2,0:T(2,128)(2,1)} %get-tuple-element.42, bf16[8,1,192,256]{3,1,2,0:T(2,128)(2,1)} %get-tuple-element.38, bf16[8,1,192,256]{3,1,2,0:T(2,128)(2,1)} %get-tuple-element.34), kind=kLoop, calls=%fused_computation.7 | loop fusion | flops 7077888 | bytes 4718592 | tf_op jit(solution)/shard_map/transpose | solution.py:218
  659.5 6.8 maximum_bitcast_fusion.2
  672.7 6.8 maximum_bitcast_fusion.3
  (179 shorter events, 172.6 us)
Async XLA Ops:
  53.5 43.0 %all-to-all-start.4 = ((bf16[8,4,192,256]{3,2,1,0:T(8,128)(2,1)}), bf16[8,4,192,256]{3,2,1,0:T(8,128)(2,1)S(1)}, u32[]{:S(2)}, u32[]{:S(2)}) async-start(bf16[8,4,192,256]{3,2,1,0:T(8,128)(2,1)} %copy.180), calls=%async_computation.4 | async-start | bytes 6291456 | tf_op jit(solution)/shard_map/all_to_all | solution.py:200
  98.3 41.6 %all-to-all-start = ((bf16[8,4,192,256]{3,2,1,0:T(8,128)(2,1)}), bf16[8,4,192,256]{3,2,1,0:T(8,128)(2,1)S(1)}, u32[]{:S(2)}, u32[]{:S(2)}) async-start(bf16[8,4,192,256]{3,2,1,0:T(8,128)(2,1)} %copy.174), calls=%async_computation | async-start | bytes 6291456 | tf_op jit(solution)/shard_map/all_to_all | solution.py:200
  141.7 41.4 %all-to-all-start.2 = ((bf16[8,4,192,256]{3,2,1,0:T(8,128)(2,1)}), bf16[8,4,192,256]{3,2,1,0:T(8,128)(2,1)S(1)}, u32[]{:S(2)}, u32[]{:S(2)}) async-start(bf16[8,4,192,256]{3,2,1,0:T(8,128)(2,1)} %copy.177), calls=%async_computation.2 | async-start | bytes 6291456 | tf_op jit(solution)/shard_map/all_to_all | solution.py:200
  149.8 38.6 %collective-permute-start.17 = (bf16[2,2,4,192,256]{4,3,2,1,0:T(8,128)(2,1)}, bf16[2,2,4,192,256]{4,3,2,1,0:T(8,128)(2,1)}, u32[]{:S(2)}, u32[]{:S(2)}) collective-permute-start(bf16[2,2,4,192,256]{4,3,2,1,0:T(8,128)(2,1)} %get-tuple-element.73), channel_id=1, source_target_pairs={{0,4},{4,8},{8,12},{1,5},{5,9},{9,13},{2,6},{6,10},{10,14},{3,7},{... | collective-permute-start | bytes 4718600 | tf_op jit(solution)/shard_map/ppermute | solution.py:126
  155.8 31.4 %collective-permute-start.16 = (bf16[1,2,4,192,256]{4,3,2,1,0:T(8,128)(2,1)}, bf16[1,2,4,192,256]{4,3,2,1,0:T(8,128)(2,1)}, u32[]{:S(2)}, u32[]{:S(2)}) collective-permute-start(bf16[1,2,4,192,256]{4,3,2,1,0:T(8,128)(2,1)} %get-tuple-element.71), channel_id=1, source_target_pairs={{12,0},{13,1},{14,2},{15,3},{28,16},{29,17},{30,18},{31,19}} | collective-permute-start | bytes 2359304 | tf_op jit(solution)/shard_map/ppermute | solution.py:127
  157.2 87.5 %collective-permute-start.19 = (bf16[2,2,4,192,256]{4,3,2,1,0:T(8,128)(2,1)}, bf16[2,2,4,192,256]{4,3,2,1,0:T(8,128)(2,1)}, u32[]{:S(2)}, u32[]{:S(2)}) collective-permute-start(bf16[2,2,4,192,256]{4,3,2,1,0:T(8,128)(2,1)} %get-tuple-element.72), channel_id=1, source_target_pairs={{4,0},{8,4},{12,8},{5,1},{9,5},{13,9},{6,2},{10,6},{14,10},{7,3},{... | collective-permute-start | bytes 4718600 | tf_op jit(solution)/shard_map/ppermute | solution.py:134
  160.6 89.7 %collective-permute-start.1 = (bf16[2,2,4,192,256]{4,3,2,1,0:T(8,128)(2,1)}, bf16[2,2,4,192,256]{4,3,2,1,0:T(8,128)(2,1)}, u32[]{:S(2)}, u32[]{:S(2)}) collective-permute-start(bf16[2,2,4,192,256]{4,3,2,1,0:T(8,128)(2,1)} %get-tuple-element.49), channel_id=1, source_target_pairs={{0,4},{4,8},{8,12},{1,5},{5,9},{9,13},{2,6},{6,10},{10,14},{3,7},{... | collective-permute-start | bytes 4718600 | tf_op jit(solution)/shard_map/ppermute | solution.py:126
  168.0 70.5 %collective-permute-start.18 = (bf16[1,2,4,192,256]{4,3,2,1,0:T(8,128)(2,1)}, bf16[1,2,4,192,256]{4,3,2,1,0:T(8,128)(2,1)}, u32[]{:S(2)}, u32[]{:S(2)}) collective-permute-start(bf16[1,2,4,192,256]{4,3,2,1,0:T(8,128)(2,1)} %get-tuple-element.70), channel_id=1, source_target_pairs={{0,12},{1,13},{2,14},{3,15},{16,28},{17,29},{18,30},{19,31}} | collective-permute-start | bytes 2359304 | tf_op jit(solution)/shard_map/ppermute | solution.py:135
  187.2 61.9 %collective-permute-start = (bf16[1,2,4,192,256]{4,3,2,1,0:T(8,128)(2,1)S(1)}, bf16[1,2,4,192,256]{4,3,2,1,0:T(8,128)(2,1)S(1)}, u32[]{:S(2)}, u32[]{:S(2)}) collective-permute-start(bf16[1,2,4,192,256]{4,3,2,1,0:T(8,128)(2,1)S(1)} %get-tuple-element.47), channel_id=1, source_target_pairs={{12,0},{13,1},{14,2},{15,3},{28,16},{29,17},{30,18},{31,19}} | collective-permute-start | bytes 2359304 | tf_op jit(solution)/shard_map/ppermute | solution.py:127
  188.5 109.6 %collective-permute-start.3 = (bf16[2,2,4,192,256]{4,3,2,1,0:T(8,128)(2,1)S(1)}, bf16[2,2,4,192,256]{4,3,2,1,0:T(8,128)(2,1)S(1)}, u32[]{:S(2)}, u32[]{:S(2)}) collective-permute-start(bf16[2,2,4,192,256]{4,3,2,1,0:T(8,128)(2,1)S(1)} %copy-done.22), channel_id=1, source_target_pairs={{4,0},{8,4},{12,8},{5,1},{9,5},{13,9},{6,2},{10,6},{14,10},{7,3},{... | collective-permute-start | bytes 4718600 | tf_op jit(solution)/shard_map/ppermute | solution.py:134
  238.4 38.7 %collective-permute-start.2 = (bf16[1,2,4,192,256]{4,3,2,1,0:T(8,128)(2,1)}, bf16[1,2,4,192,256]{4,3,2,1,0:T(8,128)(2,1)S(1)}, u32[]{:S(2)}, u32[]{:S(2)}) collective-permute-start(bf16[1,2,4,192,256]{4,3,2,1,0:T(8,128)(2,1)} %get-tuple-element.46), channel_id=1, source_target_pairs={{0,12},{1,13},{2,14},{3,15},{16,28},{17,29},{18,30},{19,31}} | collective-permute-start | bytes 2359304 | tf_op jit(solution)/shard_map/ppermute | solution.py:135
  244.7 99.0 %collective-permute-start.9 = (bf16[2,2,4,192,256]{4,3,2,1,0:T(8,128)(2,1)S(1)}, bf16[2,2,4,192,256]{4,3,2,1,0:T(8,128)(2,1)S(1)}, u32[]{:S(2)}, u32[]{:S(2)}) collective-permute-start(bf16[2,2,4,192,256]{4,3,2,1,0:T(8,128)(2,1)S(1)} %get-tuple-element.67), channel_id=1, source_target_pairs={{0,4},{4,8},{8,12},{1,5},{5,9},{9,13},{2,6},{6,10},{10,14},{3,7},{... | collective-permute-start | bytes 4718600 | tf_op jit(solution)/shard_map/ppermute | solution.py:126
  249.0 47.8 %collective-permute-start.8 = (bf16[1,2,4,192,256]{4,3,2,1,0:T(8,128)(2,1)}, bf16[1,2,4,192,256]{4,3,2,1,0:T(8,128)(2,1)}, u32[]{:S(2)}, u32[]{:S(2)}) collective-permute-start(bf16[1,2,4,192,256]{4,3,2,1,0:T(8,128)(2,1)} %get-tuple-element.65), channel_id=1, source_target_pairs={{12,0},{13,1},{14,2},{15,3},{28,16},{29,17},{30,18},{31,19}} | collective-permute-start | bytes 2359304 | tf_op jit(solution)/shard_map/ppermute | solution.py:127
  250.3 95.9 %collective-permute-start.11 = (bf16[2,2,4,192,256]{4,3,2,1,0:T(8,128)(2,1)S(1)}, bf16[2,2,4,192,256]{4,3,2,1,0:T(8,128)(2,1)S(1)}, u32[]{:S(2)}, u32[]{:S(2)}) collective-permute-start(bf16[2,2,4,192,256]{4,3,2,1,0:T(8,128)(2,1)S(1)} %get-tuple-element.66), channel_id=1, source_target_pairs={{4,0},{8,4},{12,8},{5,1},{9,5},{13,9},{6,2},{10,6},{14,10},{7,3},{... | collective-permute-start | bytes 4718600 | tf_op jit(solution)/shard_map/ppermute | solution.py:134
  277.2 54.4 %collective-permute-start.10 = (bf16[1,2,4,192,256]{4,3,2,1,0:T(8,128)(2,1)}, bf16[1,2,4,192,256]{4,3,2,1,0:T(8,128)(2,1)}, u32[]{:S(2)}, u32[]{:S(2)}) collective-permute-start(bf16[1,2,4,192,256]{4,3,2,1,0:T(8,128)(2,1)} %get-tuple-element.64), channel_id=1, source_target_pairs={{0,12},{1,13},{2,14},{3,15},{16,28},{17,29},{18,30},{19,31}} | collective-permute-start | bytes 2359304 | tf_op jit(solution)/shard_map/ppermute | solution.py:135
  296.8 50.7 %collective-permute-start.20 = (bf16[1,2,4,192,256]{4,3,2,1,0:T(8,128)(2,1)}, bf16[1,2,4,192,256]{4,3,2,1,0:T(8,128)(2,1)S(1)}, u32[]{:S(2)}, u32[]{:S(2)}) collective-permute-start(bf16[1,2,4,192,256]{4,3,2,1,0:T(8,128)(2,1)} %slice.196), channel_id=1, source_target_pairs={{12,0},{13,1},{14,2},{15,3},{28,16},{29,17},{30,18},{31,19}} | collective-permute-start | bytes 2359304 | tf_op jit(solution)/shard_map/ppermute | solution.py:127
  298.1 50.8 %collective-permute-start.22 = (bf16[1,2,4,192,256]{4,3,2,1,0:T(8,128)(2,1)}, bf16[1,2,4,192,256]{4,3,2,1,0:T(8,128)(2,1)S(1)}, u32[]{:S(2)}, u32[]{:S(2)}) collective-permute-start(bf16[1,2,4,192,256]{4,3,2,1,0:T(8,128)(2,1)} %slice.198), channel_id=1, source_target_pairs={{0,12},{1,13},{2,14},{3,15},{16,28},{17,29},{18,30},{19,31}} | collective-permute-start | bytes 2359304 | tf_op jit(solution)/shard_map/ppermute | solution.py:135
  331.6 29.5 %collective-permute-start.6 = (bf16[1,2,4,192,256]{4,3,2,1,0:T(8,128)(2,1)}, bf16[1,2,4,192,256]{4,3,2,1,0:T(8,128)(2,1)}, u32[]{:S(2)}, u32[]{:S(2)}) collective-permute-start(bf16[1,2,4,192,256]{4,3,2,1,0:T(8,128)(2,1)} %slice.172), channel_id=1, source_target_pairs={{0,12},{1,13},{2,14},{3,15},{16,28},{17,29},{18,30},{19,31}} | collective-permute-start | bytes 2359304 | tf_op jit(solution)/shard_map/ppermute | solution.py:135
  343.7 87.3 %collective-permute-start.21 = (bf16[2,2,4,192,256]{4,3,2,1,0:T(8,128)(2,1)}, bf16[2,2,4,192,256]{4,3,2,1,0:T(8,128)(2,1)}, u32[]{:S(2)}, u32[]{:S(2)}) collective-permute-start(bf16[2,2,4,192,256]{4,3,2,1,0:T(8,128)(2,1)} %get-tuple-element.19), channel_id=1, source_target_pairs={{0,4},{4,8},{8,12},{1,5},{5,9},{9,13},{2,6},{6,10},{10,14},{3,7},{... | collective-permute-start | bytes 4718600 | tf_op jit(solution)/shard_map/ppermute | solution.py:126
  346.2 84.8 %collective-permute-start.23 = (bf16[2,2,4,192,256]{4,3,2,1,0:T(8,128)(2,1)S(1)}, bf16[2,2,4,192,256]{4,3,2,1,0:T(8,128)(2,1)}, u32[]{:S(2)}, u32[]{:S(2)}) collective-permute-start(bf16[2,2,4,192,256]{4,3,2,1,0:T(8,128)(2,1)S(1)} %get-tuple-element.21), channel_id=1, source_target_pairs={{4,0},{8,4},{12,8},{5,1},{9,5},{13,9},{6,2},{10,6},{14,10},{7,3},{... | collective-permute-start | bytes 4718600 | tf_op jit(solution)/shard_map/ppermute | solution.py:134
  347.5 85.6 %collective-permute-start.7 = (bf16[2,2,4,192,256]{4,3,2,1,0:T(8,128)(2,1)}, bf16[2,2,4,192,256]{4,3,2,1,0:T(8,128)(2,1)}, u32[]{:S(2)}, u32[]{:S(2)}) collective-permute-start(bf16[2,2,4,192,256]{4,3,2,1,0:T(8,128)(2,1)} %get-tuple-element.15), channel_id=1, source_target_pairs={{4,0},{8,4},{12,8},{5,1},{9,5},{13,9},{6,2},{10,6},{14,10},{7,3},{... | collective-permute-start | bytes 4718600 | tf_op jit(solution)/shard_map/ppermute | solution.py:134
  348.9 84.3 %collective-permute-start.5 = (bf16[2,2,4,192,256]{4,3,2,1,0:T(8,128)(2,1)}, bf16[2,2,4,192,256]{4,3,2,1,0:T(8,128)(2,1)}, u32[]{:S(2)}, u32[]{:S(2)}) collective-permute-start(bf16[2,2,4,192,256]{4,3,2,1,0:T(8,128)(2,1)} %get-tuple-element.13), channel_id=1, source_target_pairs={{0,4},{4,8},{8,12},{1,5},{5,9},{9,13},{2,6},{6,10},{10,14},{3,7},{... | collective-permute-start | bytes 4718600 | tf_op jit(solution)/shard_map/ppermute | solution.py:126
  361.1 69.9 %collective-permute-start.4 = (bf16[1,2,4,192,256]{4,3,2,1,0:T(8,128)(2,1)S(1)}, bf16[1,2,4,192,256]{4,3,2,1,0:T(8,128)(2,1)S(1)}, u32[]{:S(2)}, u32[]{:S(2)}) collective-permute-start(bf16[1,2,4,192,256]{4,3,2,1,0:T(8,128)(2,1)S(1)} %slice.169), channel_id=1, source_target_pairs={{12,0},{13,1},{14,2},{15,3},{28,16},{29,17},{30,18},{31,19}} | collective-permute-start | bytes 2359304 | tf_op jit(solution)/shard_map/ppermute | solution.py:127
  362.4 70.7 %copy-start.18 = (bf16[2,4,4,192,256]{4,3,2,1,0:T(8,128)(2,1)S(1)}, bf16[2,4,4,192,256]{4,3,2,1,0:T(8,128)(2,1)}, u32[]{:S(2)}) copy-start(bf16[2,4,4,192,256]{4,3,2,1,0:T(8,128)(2,1)} %get-tuple-element.14) | copy-start | bytes 9437188
  363.9 69.3 %copy-start.17 = (bf16[2,4,4,192,256]{4,3,2,1,0:T(8,128)(2,1)S(1)}, bf16[2,4,4,192,256]{4,3,2,1,0:T(8,128)(2,1)}, u32[]{:S(2)}) copy-start(bf16[2,4,4,192,256]{4,3,2,1,0:T(8,128)(2,1)} %get-tuple-element.20) | copy-start | bytes 9437188
  442.0 96.8 %all-to-all-start.5 = ((bf16[8,4,192,256]{3,1,2,0:T(4,128)(2,1)}), bf16[8,4,192,256]{3,1,2,0:T(4,128)(2,1)}, u32[]{:S(2)}, u32[]{:S(2)}) async-start(bf16[8,4,192,256]{3,1,2,0:T(4,128)(2,1)} %copy.182), calls=%async_computation.5 | async-start | bytes 6291456 | tf_op jit(solution)/shard_map/all_to_all | solution.py:214
  469.1 64.9 %collective-permute-start.13 = (bf16[2,2,4,192,256]{4,3,2,1,0:T(8,128)(2,1)S(1)}, bf16[2,2,4,192,256]{4,3,2,1,0:T(8,128)(2,1)S(1)}, u32[]{:S(2)}, u32[]{:S(2)}) collective-permute-start(bf16[2,2,4,192,256]{4,3,2,1,0:T(8,128)(2,1)S(1)} %get-tuple-element.16), channel_id=1, source_target_pairs={{0,4},{4,8},{8,12},{1,5},{5,9},{9,13},{2,6},{6,10},{10,14},{3,7},{... | collective-permute-start | bytes 4718600 | tf_op jit(solution)/shard_map/ppermute | solution.py:126
  475.8 58.2 %collective-permute-start.15 = (bf16[2,2,4,192,256]{4,3,2,1,0:T(8,128)(2,1)S(1)}, bf16[2,2,4,192,256]{4,3,2,1,0:T(8,128)(2,1)S(1)}, u32[]{:S(2)}, u32[]{:S(2)}) collective-permute-start(bf16[2,2,4,192,256]{4,3,2,1,0:T(8,128)(2,1)S(1)} %get-tuple-element.18), channel_id=1, source_target_pairs={{4,0},{8,4},{12,8},{5,1},{9,5},{13,9},{6,2},{10,6},{14,10},{7,3},{... | collective-permute-start | bytes 4718600 | tf_op jit(solution)/shard_map/ppermute | solution.py:134
  477.4 56.5 %collective-permute-start.12 = (bf16[1,2,4,192,256]{4,3,2,1,0:T(8,128)(2,1)S(1)}, bf16[1,2,4,192,256]{4,3,2,1,0:T(8,128)(2,1)S(1)}, u32[]{:S(2)}, u32[]{:S(2)}) collective-permute-start(bf16[1,2,4,192,256]{4,3,2,1,0:T(8,128)(2,1)S(1)} %slice.183), channel_id=1, source_target_pairs={{12,0},{13,1},{14,2},{15,3},{28,16},{29,17},{30,18},{31,19}} | collective-permute-start | bytes 2359304 | tf_op jit(solution)/shard_map/ppermute | solution.py:127
  478.7 55.2 %collective-permute-start.14 = (bf16[1,2,4,192,256]{4,3,2,1,0:T(8,128)(2,1)S(1)}, bf16[1,2,4,192,256]{4,3,2,1,0:T(8,128)(2,1)S(1)}, u32[]{:S(2)}, u32[]{:S(2)}) collective-permute-start(bf16[1,2,4,192,256]{4,3,2,1,0:T(8,128)(2,1)S(1)} %slice.185), channel_id=1, source_target_pairs={{0,12},{1,13},{2,14},{3,15},{16,28},{17,29},{18,30},{19,31}} | collective-permute-start | bytes 2359304 | tf_op jit(solution)/shard_map/ppermute | solution.py:135
  538.9 41.7 %all-to-all-start.3 = ((bf16[8,4,192,256]{3,1,2,0:T(4,128)(2,1)}), bf16[8,4,192,256]{3,1,2,0:T(4,128)(2,1)S(1)}, u32[]{:S(2)}, u32[]{:S(2)}) async-start(bf16[8,4,192,256]{3,1,2,0:T(4,128)(2,1)} %copy.179), calls=%async_computation.3 | async-start | bytes 6291456 | tf_op jit(solution)/shard_map/all_to_all | solution.py:214
  580.6 42.6 %all-to-all-start.1 = ((bf16[8,4,192,256]{3,1,2,0:T(4,128)(2,1)}), bf16[8,4,192,256]{3,1,2,0:T(4,128)(2,1)}, u32[]{:S(2)}, u32[]{:S(2)}) async-start(bf16[8,4,192,256]{3,1,2,0:T(4,128)(2,1)} %copy.176), calls=%async_computation.1 | async-start | bytes 6291456 | tf_op jit(solution)/shard_map/all_to_all | solution.py:214
  (29 other events, 277.1 us)

commit v2 on v1

--- a/solution.py
+++ b/solution.py
@@ -7,6 +7,7 @@
 from jax.experimental import pallas as pl
 from jax.experimental.pallas import tpu as pltpu
 from jax.sharding import PartitionSpec as P
+
 
 DH = 128
 GROUPS = 3
@@ -138,7 +139,6 @@
 
 
 def clip_plan(clip_lengths, block_rows, side_rows, enc, ctx):
-    length = block_rows * enc * ctx
     window = block_rows + 2 * side_rows
     ends = jnp.cumsum(clip_lengths).astype(jnp.int32)
     starts = ends - clip_lengths
@@ -179,44 +179,114 @@
     return plan, row_ids[:, :, None], key_ids[:, None, :], before, after
 
 
+def pack_kernel(*refs):
+    *arrays, packed = refs
+    for a, ref in enumerate(arrays):
+        packed[0, a] = ref[...]
+
+
+def pack(arrays, group, team, wide):
+    rows = arrays[0].shape[0]
+    return pl.pallas_call(
+        pack_kernel,
+        grid=(team,),
+        in_specs=[pl.BlockSpec((rows, wide), lambda d: (0, d * GROUPS + group))] * len(arrays),
+        out_specs=pl.BlockSpec((1, len(arrays), rows, wide), lambda d: (d, 0, 0, 0)),
+        out_shape=jax.ShapeDtypeStruct((team, len(arrays), rows, wide), arrays[0].dtype),
+        cost_estimate=pl.CostEstimate(
+            flops=0, bytes_accessed=4 * team * len(arrays) * rows * wide, transcendentals=0
+        ),
+    )(*arrays)
+
+
+def unpack_kernel(packed, *refs):
+    outs = refs[len(refs) - packed.shape[1]:]
+    for a, ref in enumerate(outs):
+        ref[...] = packed[0, a]
+
+
+def unpack(packed, held, group):
+    team, arrays, rows, wide = packed.shape
+    return pl.pallas_call(
+        unpack_kernel,
+        grid=(team,),
+        in_specs=[pl.BlockSpec((1, arrays, rows, wide), lambda d: (d, 0, 0, 0))]
+        + [pl.BlockSpec(memory_space=pl.ANY)] * len(held),
+        out_specs=[pl.BlockSpec((rows, wide), lambda d: (0, d * GROUPS + group))] * arrays,
+        out_shape=[
+            jax.ShapeDtypeStruct((rows, team * GROUPS * wide), packed.dtype)
+        ] * arrays,
+        input_output_aliases={1 + a: a for a in range(len(held))},
+        cost_estimate=pl.CostEstimate(
+            flops=0, bytes_accessed=4 * packed.size, transcendentals=0
+        ),
+    )(packed, *held)
+
+
+def merge_kernel(side, choice, own, low, high, merged):
+    t = pl.program_id(1)
+
+    @pl.when(t < side)
+    def _():
+        for a in range(own.shape[2]):
+            merged[0, a] = jnp.where(choice[0, 0] == 1, low[0, 0, a], own[0, 0, a])
+
+    @pl.when(t >= side)
+    def _():
+        for a in range(own.shape[2]):
+            merged[0, a] = jnp.where(choice[0, 0] == 2, high[0, 0, a], own[0, 0, a])
+
+
+def merge(choice, own, low, high):
+    enc, tp, arrays, rows, wide = own.shape
+    side = low.shape[1]
+    part = (1, 1, arrays, rows, wide)
+    return pl.pallas_call(
+        functools.partial(merge_kernel, side),
+        grid=(enc, tp),
+        in_specs=[
+            pl.BlockSpec((1, 1, rows, 1), lambda e, t: (e, t, 0, 0)),
+            pl.BlockSpec(part, lambda e, t: (e, t, 0, 0, 0)),
+            pl.BlockSpec(part, lambda e, t: (e, jnp.minimum(t, side - 1), 0, 0, 0)),
+            pl.BlockSpec(part, lambda e, t: (e, jnp.maximum(t - tp + side, 0), 0, 0, 0)),
+        ],
+        out_specs=pl.BlockSpec((1, arrays, rows, wide), lambda e, t: (e * tp + t, 0, 0, 0)),
+        out_shape=jax.ShapeDtypeStruct((enc * tp, arrays, rows, wide), own.dtype),
+        cost_estimate=pl.CostEstimate(
+            flops=own.size, bytes_accessed=6 * own.size, transcendentals=0
+        ),
+    )(choice, own, low, high)
+
+
 def per_device(query_rows, key_rows, value_rows, out_grad, clip_lengths):
     enc, ctx, tp = (lax.axis_size(a) for a in ("enc", "ctx", "tp"))
     team = enc * tp
     rows, features = query_rows.shape
     wide = features // (team * GROUPS)
     side = tp // 2
+    arrays = (query_rows, key_rows, value_rows, out_grad)
+    axes = ("enc", "tp")
+    exchange = functools.partial(
+        lax.all_to_all, axis_name=axes, split_axis=0, concat_axis=0, tiled=True
+    )
+    outs = ()
     plan, row_ids, key_ids, before, after = clip_plan(
         clip_lengths, rows * tp, rows * side, enc, ctx
     )
-    before = before.reshape(enc, tp, 1, rows, 1)[:, :side]
-    after = after.reshape(enc, tp, 1, rows, 1)[:, tp - side :]
-    arrays = [
-        a.reshape(rows, team, GROUPS, wide) for a in (query_rows, key_rows, value_rows, out_grad)
-    ]
-    axes = ("enc", "tp")
-    results = []
+    choice = jnp.where(before, 1, jnp.where(after, 2, 0)).astype(jnp.int32)
+    choice = choice.reshape(enc, tp, rows, 1)
     for g in range(GROUPS):
-        sent = jnp.stack([a[:, :, g].transpose(1, 0, 2) for a in arrays], axis=1)
-        own = lax.all_to_all(sent, axes, split_axis=0, concat_axis=0, tiled=True)
-        own = own.reshape(enc, tp, 4, rows, wide)
+        sent = pack(arrays, g, team, wide)
+        own = exchange(sent).reshape(enc, tp, 4, rows, wide)
         low = from_previous(own[:, tp - side :])
         high = from_next(own[:, :side])
         low_out, own_out, high_out = attention(plan, low, own, high, row_ids, key_ids)
         back_low = from_previous(high_out)
         back_high = from_next(low_out)
-        total = jnp.concatenate(
-            [
-                jnp.where(before, back_low, own_out[:, :side]),
-                jnp.where(after, back_high, own_out[:, tp - side :]),
-            ],
-            axis=1,
-        ).reshape(team, 4, rows, wide)
-        results.append(lax.all_to_all(total, axes, split_axis=0, concat_axis=0, tiled=True))
-    done = []
-    for a in range(4):
-        joined = jnp.stack([r[:, a] for r in results], axis=1)
-        done.append(joined.transpose(2, 0, 1, 3).reshape(rows, features))
-    return tuple(done)
+        total = merge(choice, own_out, back_low, back_high)
+        total = exchange(total)
+        outs = unpack(total, outs, g)
+    return tuple(outs)
 
 
 def solution(mesh):

time: 692 us -> 539 us (0.78)
  local copies, waits for them, and re-layouts: 154 us -> 25.5 us
  Pallas kernels: 66.9 us -> 129 us
  waiting for transfers between devices: 289 us -> 246 us
  other arithmetic: 48.5 us -> 21.8 us
  starting transfers between devices: 126 us -> 113 us
    ppermute x6, waiting for transfers between devices: 50.3 us -> 163 us  [from_next(): wrapped = lax.ppermute(x[1:], 'ctx', [(0, count - 1)])]
    ppermute x6, waiting for transfers between devices: 112 us -> 2.5 us  [from_previous(): wrapped = lax.ppermute(x[:-1], 'ctx', [(count - 1, 0)])]
    pallas_call x0 -> x9, Pallas kernels: none -> 59.5 us  [the longest x3 22.2 us: merge(): pl.pallas_call(functools.partial(merge_kernel, side), grid=(enc, tp), in_...]
    all_to_all x6, waiting for transfers between devices: 124 us -> 69.8 us  [the longest x3 44.2 us: per_device(): own = exchange(sent).reshape(enc, tp, 4, rows, wide)]
    reshape x13 -> x1, local copies, waits for them, and re-layouts: 55 us -> 1.55 us  [per_device(): choice = choice.reshape(enc, tp, rows, 1)]
    slice x7 -> x0, local copies, waits for them, and re-layouts: 49.7 us -> none  [the longest x3 30.6 us: per_device(): joined = jnp.stack([r[:, a] for r in results], axis=1)]
    transpose x4 -> x0, other arithmetic: 26.1 us -> none  [per_device(): done.append(joined.transpose(2, 0, 1, 3).reshape(rows, features))]
    ppermute x6, starting transfers between devices: 57.2 us -> 34.5 us  [from_next(): wrapped = lax.ppermute(x[1:], 'ctx', [(0, count - 1)])]
  transfers between devices with their start and end apart: 30 -> 30, of which waited for: 10 -> 10; matrix products, arithmetic and copies ran while one was open for 10% -> 8% of each run, Pallas kernels for 10% -> 22%
where the time goes in v2:
time: 539 us; the launch traced here: 536 us
  waiting for transfers between devices  246 us (46%)
  Pallas kernels  129 us (24%)
  starting transfers between devices  113 us (21%)
  local copies, waits for them, and re-layouts  25.5 us (5%)
  other arithmetic  21.8 us (4%)
    ppermute x6, waiting for transfers between devices, from_next(): wrapped = lax.ppermute(x[1:], 'ctx', [(0, count - 1)])  163 us
    pallas_call x3, Pallas kernels, attention(): pl.pallas_call(attention_kernel, grid_spec=grid_spec, out_shape=[jax.Shap...  69.9 us
    all_to_all x3, waiting for transfers between devices, per_device(): own = exchange(sent).reshape(enc, tp, 4, rows, wide)  44.2 us
    ppermute x6, starting transfers between devices, from_previous(): got = lax.ppermute(x, 'ctx', [(i, i + 1) for i in range(count - 1)])  37.7 us
    ppermute x6, starting transfers between devices, from_next(): wrapped = lax.ppermute(x[1:], 'ctx', [(0, count - 1)])  34.5 us
    all_to_all x3, waiting for transfers between devices, per_device(): total = exchange(total)  25.5 us
    pallas_call x3, Pallas kernels, merge(): pl.pallas_call(functools.partial(merge_kernel, side), grid=(enc, tp), in_...  22.2 us
    pallas_call x3, Pallas kernels, pack(): pl.pallas_call(pack_kernel, grid=(team,), in_specs=[pl.BlockSpec((rows, w...  18.9 us
  transfers between devices with their start and end apart: 30, of which 10 were waited for; matrix products, arithmetic and copies ran while one was open for 8% of the time, Pallas kernels for 22%

profile of v2, /device:TPU:0, one launch (start us, length us, event | category | flops | bytes accessed | tf_op | source)
XLA Modules:
  0.0 536.1 jit_solution(5586570831697688662)
XLA Ops:
  0.6 6.3 %shard_map.90 = bf16[8,4,192,256]{3,2,1,0:T(8,128)(2,1)} custom-call(bf16[192,6144]{1,0:T(8,128)(2,1)} %refs_0_.5, bf16[192,6144]{1,0:T(8,128)(2,1)} %refs_1_.5, bf16[192,6144]{1,0:T(8,128)(2,1)} %refs_2_.5, bf16[192,6144]{1,0:T(8,128)(2,1)} %refs_3_.5), custom_call_target="tpu_custom_call" | custom-call | bytes 6291456 | tf_op jit(solution)/shard_map/pallas_call | solution.py:190
  6.9 5.2 all-to-all-start.4
  12.1 6.3 %shard_map.87 = bf16[8,4,192,256]{3,2,1,0:T(8,128)(2,1)} custom-call(bf16[192,6144]{1,0:T(8,128)(2,1)} %refs_0_.5, bf16[192,6144]{1,0:T(8,128)(2,1)} %refs_1_.5, bf16[192,6144]{1,0:T(8,128)(2,1)} %refs_2_.5, bf16[192,6144]{1,0:T(8,128)(2,1)} %refs_3_.5), custom_call_target="tpu_custom_call" | custom-call | bytes 6291456 | tf_op jit(solution)/shard_map/pallas_call | solution.py:190
  18.8 31.2 %all-to-all-done.4 = bf16[8,4,192,256]{3,2,1,0:T(8,128)(2,1)S(1)} async-done(((bf16[8,4,192,256]{3,2,1,0:T(8,128)(2,1)}), bf16[8,4,192,256]{3,2,1,0:T(8,128)(2,1)S(1)}, u32[]{:S(2)}, u32[]{:S(2)}) %all-to-all-start.4) | async-done | bytes 3145760 | tf_op jit(solution)/shard_map/all_to_all | solution.py:280
  61.2 5.7 %collective-permute-start.17 = (bf16[2,2,4,192,256]{4,3,2,1,0:T(8,128)(2,1)}, bf16[2,2,4,192,256]{4,3,2,1,0:T(8,128)(2,1)}, u32[]{:S(2)}, u32[]{:S(2)}) collective-permute-start(bf16[2,2,4,192,256]{4,3,2,1,0:T(8,128)(2,1)} %get-tuple-element.51), channel_id=1, source_target_pairs={{0,4},{4,8},{8,12},{1,5},{5,9},{9,13},{2,6},{6,10},{10,14},{3,7},{... | collective-permute-start | bytes 4718600 | tf_op jit(solution)/shard_map/ppermute | solution.py:127
  66.9 6.3 %shard_map.84 = bf16[8,4,192,256]{3,2,1,0:T(8,128)(2,1)} custom-call(bf16[192,6144]{1,0:T(8,128)(2,1)} %refs_0_.5, bf16[192,6144]{1,0:T(8,128)(2,1)} %refs_1_.5, bf16[192,6144]{1,0:T(8,128)(2,1)} %refs_2_.5, bf16[192,6144]{1,0:T(8,128)(2,1)} %refs_3_.5), custom_call_target="tpu_custom_call" | custom-call | bytes 6291456 | tf_op jit(solution)/shard_map/pallas_call | solution.py:190
  80.1 13.0 %all-to-all-done.2 = bf16[8,4,192,256]{3,2,1,0:T(8,128)(2,1)S(1)} async-done(((bf16[8,4,192,256]{3,2,1,0:T(8,128)(2,1)}), bf16[8,4,192,256]{3,2,1,0:T(8,128)(2,1)S(1)}, u32[]{:S(2)}, u32[]{:S(2)}) %all-to-all-start.2) | async-done | bytes 3145760 | tf_op jit(solution)/shard_map/all_to_all | solution.py:280
  93.1 4.5 all-to-all-start
  104.8 12.1 %collective-permute-done.18 = bf16[1,2,4,192,256]{4,3,2,1,0:T(8,128)(2,1)} collective-permute-done((bf16[1,2,4,192,256]{4,3,2,1,0:T(8,128)(2,1)}, bf16[1,2,4,192,256]{4,3,2,1,0:T(8,128)(2,1)}, u32[]{:S(2)}, u32[]{:S(2)}) %collective-permute-start.18) | collective-permute-done | bytes 786464 | tf_op jit(solution)/shard_map/ppermute | solution.py:136
  116.9 7.1 %collective-permute-start.10 = (bf16[1,2,4,192,256]{4,3,2,1,0:T(8,128)(2,1)S(1)}, bf16[1,2,4,192,256]{4,3,2,1,0:T(8,128)(2,1)}, u32[]{:S(2)}, u32[]{:S(2)}) collective-permute-start(bf16[1,2,4,192,256]{4,3,2,1,0:T(8,128)(2,1)S(1)} %get-tuple-element.52), channel_id=1, source_target_pairs={{0,12},{1,13},{2,14},{3,15},{16,28},{17,29},{18,30},{19,31}} | collective-permute-start | bytes 2359304 | tf_op jit(solution)/shard_map/ppermute | solution.py:136
  127.1 23.3 %shard_map.91 = (bf16[2,2,4,192,256]{4,3,2,1,0:T(8,128)(2,1)S(1)}, bf16[2,4,4,192,256]{4,3,2,1,0:T(8,128)(2,1)}, bf16[2,2,4,192,256]{4,3,2,1,0:T(8,128)(2,1)S(1)}) custom-call(s32[2,2,6]{2,1,0:T(2,128)S(1)} %pad_add_fusion.plan_ref, bf16[2,2,4,192,256]{4,3,2,1,0:T(8,128)(2,1)S(1)} %pad_select_fusion.3.low_ref, bf16[2,4,4,192,256]{4,3,2,1,0:T(8,128)(2,1)} %bitcast.19, ...), custom_call_target="tpu_custom_call" | custom-call | flops 6039797760 | bytes 12582912 | tf_op jit(solution)/shard_map/pallas_call | solution.py:112
  151.7 5.7 %collective-permute-start.21 = (bf16[2,2,4,192,256]{4,3,2,1,0:T(8,128)(2,1)S(1)}, bf16[2,2,4,192,256]{4,3,2,1,0:T(8,128)(2,1)}, u32[]{:S(2)}, u32[]{:S(2)}) collective-permute-start(bf16[2,2,4,192,256]{4,3,2,1,0:T(8,128)(2,1)S(1)} %get-tuple-element.28), channel_id=1, source_target_pairs={{0,4},{4,8},{8,12},{1,5},{5,9},{9,13},{2,6},{6,10},{10,14},{3,7},{... | collective-permute-start | bytes 4718600 | tf_op jit(solution)/shard_map/ppermute | solution.py:127
  160.8 6.2 %collective-permute-start.22 = (bf16[1,2,4,192,256]{4,3,2,1,0:T(8,128)(2,1)}, bf16[1,2,4,192,256]{4,3,2,1,0:T(8,128)(2,1)}, u32[]{:S(2)}, u32[]{:S(2)}) collective-permute-start(bf16[1,2,4,192,256]{4,3,2,1,0:T(8,128)(2,1)} %slice.81), channel_id=1, source_target_pairs={{0,12},{1,13},{2,14},{3,15},{16,28},{17,29},{18,30},{19,31}} | collective-permute-start | bytes 2359304 | tf_op jit(solution)/shard_map/ppermute | solution.py:136
  176.6 62.8 %collective-permute-done.22 = bf16[1,2,4,192,256]{4,3,2,1,0:T(8,128)(2,1)} collective-permute-done((bf16[1,2,4,192,256]{4,3,2,1,0:T(8,128)(2,1)}, bf16[1,2,4,192,256]{4,3,2,1,0:T(8,128)(2,1)}, u32[]{:S(2)}, u32[]{:S(2)}) %collective-permute-start.22) | collective-permute-done | bytes 786464 | tf_op jit(solution)/shard_map/ppermute | solution.py:136
  247.8 8.4 %collective-permute-start.2 = (bf16[1,2,4,192,256]{4,3,2,1,0:T(8,128)(2,1)}, bf16[1,2,4,192,256]{4,3,2,1,0:T(8,128)(2,1)}, u32[]{:S(2)}, u32[]{:S(2)}) collective-permute-start(bf16[1,2,4,192,256]{4,3,2,1,0:T(8,128)(2,1)} %get-tuple-element.56), channel_id=1, source_target_pairs={{0,12},{1,13},{2,14},{3,15},{16,28},{17,29},{18,30},{19,31}} | collective-permute-start | bytes 2359304 | tf_op jit(solution)/shard_map/ppermute | solution.py:136
  257.5 7.4 %shard_map.92 = bf16[8,4,192,256]{3,2,1,0:T(8,128)(2,1)} custom-call(s32[2,4,192,1]{3,2,1,0:T(8,128)} %reshape.306.choice, bf16[2,4,4,192,256]{4,3,2,1,0:T(8,128)(2,1)} %get-tuple-element.27.own, bf16[2,2,4,192,256]{4,3,2,1,0:T(8,128)(2,1)} %pad_select_fusion.1.low, bf16[2,2,4,192,256]{4,3,2,1,0:T(8,128)(2,1)} %pad_select_fusion.high), custom_call_target="tpu_custom_call" | custom-call | flops 1572864 | bytes 9437184 | tf_op jit(solution)/shard_map/pallas_call | solution.py:244
  269.9 23.3 %shard_map.88 = (bf16[2,2,4,192,256]{4,3,2,1,0:T(8,128)(2,1)S(1)}, bf16[2,4,4,192,256]{4,3,2,1,0:T(8,128)(2,1)}, bf16[2,2,4,192,256]{4,3,2,1,0:T(8,128)(2,1)S(1)}) custom-call(s32[2,2,6]{2,1,0:T(2,128)S(1)} %pad_add_fusion.plan_ref, bf16[2,2,4,192,256]{4,3,2,1,0:T(8,128)(2,1)S(1)} %pad_select_fusion.7.low_ref, bf16[2,4,4,192,256]{4,3,2,1,0:T(8,128)(2,1)} %bitcast.16, ...), custom_call_target="tpu_custom_call" | custom-call | flops 6039797760 | bytes 12582912 | tf_op jit(solution)/shard_map/pallas_call | solution.py:112
  294.5 8.0 %collective-permute-start.13 = (bf16[2,2,4,192,256]{4,3,2,1,0:T(8,128)(2,1)S(1)}, bf16[2,2,4,192,256]{4,3,2,1,0:T(8,128)(2,1)S(1)}, u32[]{:S(2)}, u32[]{:S(2)}) collective-permute-start(bf16[2,2,4,192,256]{4,3,2,1,0:T(8,128)(2,1)S(1)} %get-tuple-element.25), channel_id=1, source_target_pairs={{0,4},{4,8},{8,12},{1,5},{5,9},{9,13},{2,6},{6,10},{10,14},{3,7},{... | collective-permute-start | bytes 4718600 | tf_op jit(solution)/shard_map/ppermute | solution.py:127
  302.5 4.2 collective-permute-start.14
  310.7 43.4 %collective-permute-done.14 = bf16[1,2,4,192,256]{4,3,2,1,0:T(8,128)(2,1)S(1)} collective-permute-done((bf16[1,2,4,192,256]{4,3,2,1,0:T(8,128)(2,1)S(1)}, bf16[1,2,4,192,256]{4,3,2,1,0:T(8,128)(2,1)S(1)}, u32[]{:S(2)}, u32[]{:S(2)}) %collective-permute-start.14) | collective-permute-done | bytes 786464 | tf_op jit(solution)/shard_map/ppermute | solution.py:136
  360.8 7.4 %shard_map.89 = bf16[8,4,192,256]{3,2,1,0:T(8,128)(2,1)} custom-call(s32[2,4,192,1]{3,2,1,0:T(8,128)} %reshape.306.choice, bf16[2,4,4,192,256]{4,3,2,1,0:T(8,128)(2,1)} %get-tuple-element.24.own, bf16[2,2,4,192,256]{4,3,2,1,0:T(8,128)(2,1)} %pad_select_fusion.5.low, bf16[2,2,4,192,256]{4,3,2,1,0:T(8,128)(2,1)} %pad_select_fusion.4.high), custom_call_target="tpu_custom_call" | custom-call | flops 1572864 | bytes 9437184 | tf_op jit(solution)/shard_map/pallas_call | solution.py:244
  369.8 4.7 all-to-all-start.3
  376.6 10.7 %collective-permute-done.1 = bf16[2,2,4,192,256]{4,3,2,1,0:T(8,128)(2,1)} collective-permute-done((bf16[2,2,4,192,256]{4,3,2,1,0:T(8,128)(2,1)}, bf16[2,2,4,192,256]{4,3,2,1,0:T(8,128)(2,1)}, u32[]{:S(2)}, u32[]{:S(2)}) %collective-permute-start.1) | collective-permute-done | bytes 1572896 | tf_op jit(solution)/shard_map/ppermute | solution.py:127
  388.5 23.3 %shard_map.85 = (bf16[2,2,4,192,256]{4,3,2,1,0:T(8,128)(2,1)S(1)}, bf16[2,4,4,192,256]{4,3,2,1,0:T(8,128)(2,1)}, bf16[2,2,4,192,256]{4,3,2,1,0:T(8,128)(2,1)S(1)}) custom-call(s32[2,2,6]{2,1,0:T(2,128)S(1)} %pad_add_fusion.plan_ref, bf16[2,2,4,192,256]{4,3,2,1,0:T(8,128)(2,1)S(1)} %pad_select_fusion.11.low_ref, bf16[2,4,4,192,256]{4,3,2,1,0:T(8,128)(2,1)} %bitcast.6.own_ref, ...), custom_call_target="tpu_custom_call" | custom-call | flops 6039797760 | bytes 12582912 | tf_op jit(solution)/shard_map/pallas_call | solution.py:112
  413.1 13.2 %collective-permute-start.5 = (bf16[2,2,4,192,256]{4,3,2,1,0:T(8,128)(2,1)S(1)}, bf16[2,2,4,192,256]{4,3,2,1,0:T(8,128)(2,1)S(1)}, u32[]{:S(2)}, u32[]{:S(2)}) collective-permute-start(bf16[2,2,4,192,256]{4,3,2,1,0:T(8,128)(2,1)S(1)} %get-tuple-element.22), channel_id=1, source_target_pairs={{0,4},{4,8},{8,12},{1,5},{5,9},{9,13},{2,6},{6,10},{10,14},{3,7},{... | collective-permute-start | bytes 4718600 | tf_op jit(solution)/shard_map/ppermute | solution.py:127
  426.4 4.3 collective-permute-start.6
  432.1 44.4 %collective-permute-done.6 = bf16[1,2,4,192,256]{4,3,2,1,0:T(8,128)(2,1)S(1)} collective-permute-done((bf16[1,2,4,192,256]{4,3,2,1,0:T(8,128)(2,1)S(1)}, bf16[1,2,4,192,256]{4,3,2,1,0:T(8,128)(2,1)S(1)}, u32[]{:S(2)}, u32[]{:S(2)}) %collective-permute-start.6) | collective-permute-done | bytes 786464 | tf_op jit(solution)/shard_map/ppermute | solution.py:136
  479.5 7.4 %shard_map.86 = bf16[8,4,192,256]{3,2,1,0:T(8,128)(2,1)} custom-call(s32[2,4,192,1]{3,2,1,0:T(8,128)} %reshape.306.choice, bf16[2,4,4,192,256]{4,3,2,1,0:T(8,128)(2,1)} %get-tuple-element.21.own, bf16[2,2,4,192,256]{4,3,2,1,0:T(8,128)(2,1)} %pad_select_fusion.9.low, bf16[2,2,4,192,256]{4,3,2,1,0:T(8,128)(2,1)} %pad_select_fusion.8.high), custom_call_target="tpu_custom_call" | custom-call | flops 1572864 | bytes 9437184 | tf_op jit(solution)/shard_map/pallas_call | solution.py:244
  490.6 6.1 %shard_map.93 = (bf16[192,6144]{1,0:T(8,128)(2,1)}, bf16[192,6144]{1,0:T(8,128)(2,1)}, bf16[192,6144]{1,0:T(8,128)(2,1)}, bf16[192,6144]{1,0:T(8,128)(2,1)}) custom-call(bf16[8,4,192,256]{3,2,1,0:T(8,128)(2,1)} %copy-done.2), custom_call_target="tpu_custom_call" | custom-call | bytes 6291456 | tf_op jit(solution)/shard_map/pallas_call | solution.py:210
  496.7 6.1 %shard_map.94 = (bf16[192,6144]{1,0:T(8,128)(2,1)}, bf16[192,6144]{1,0:T(8,128)(2,1)}, bf16[192,6144]{1,0:T(8,128)(2,1)}, bf16[192,6144]{1,0:T(8,128)(2,1)}) custom-call(bf16[8,4,192,256]{3,2,1,0:T(8,128)(2,1)} %all-to-all-done.3.packed, ...), custom_call_target="tpu_custom_call", output_to_operand_aliasing={{0}: (1, {}), {1}: (2, {}), {2}: (3, {}), {3}: (4, {})} | custom-call | bytes 6291456 | tf_op jit(solution)/shard_map/pallas_call | solution.py:210
  502.8 25.5 %all-to-all-done.1.packed = bf16[8,4,192,256]{3,2,1,0:T(8,128)(2,1)S(1)} async-done(((bf16[8,4,192,256]{3,2,1,0:T(8,128)(2,1)}), bf16[8,4,192,256]{3,2,1,0:T(8,128)(2,1)S(1)}, u32[]{:S(2)}, u32[]{:S(2)}) %all-to-all-start.1) | async-done | bytes 3145760 | tf_op jit(solution)/shard_map/all_to_all | solution.py:287
  530.0 6.1 %shard_map.95 = (bf16[192,6144]{1,0:T(8,128)(2,1)}, bf16[192,6144]{1,0:T(8,128)(2,1)}, bf16[192,6144]{1,0:T(8,128)(2,1)}, bf16[192,6144]{1,0:T(8,128)(2,1)}) custom-call(bf16[8,4,192,256]{3,2,1,0:T(8,128)(2,1)} %copy-done.3, bf16[192,6144]{1,0:T(8,128)(2,1)} %get-tuple-element.34.refs_0_, ...), custom_call_target="tpu_custom_call", output_to_operand_aliasing={{0}: (1, {}), {1}: (2, {}), {2}: (3, {}), {3}: (4, {})} | custom-call | bytes 6291456 | tf_op jit(solution)/shard_map/pallas_call | solution.py:210
  (95 shorter events, 85.4 us)
Async XLA Ops:
  6.9 43.0 %all-to-all-start.4 = ((bf16[8,4,192,256]{3,2,1,0:T(8,128)(2,1)}), bf16[8,4,192,256]{3,2,1,0:T(8,128)(2,1)S(1)}, u32[]{:S(2)}, u32[]{:S(2)}) async-start(bf16[8,4,192,256]{3,2,1,0:T(8,128)(2,1)} %shard_map.90), calls=%async_computation.4 | async-start | bytes 6291456 | tf_op jit(solution)/shard_map/all_to_all | solution.py:280
  12.1 6.3 %copy-start.4 = (s32[16]{0:T(128)S(1)}, s32[16]{0:T(128)}, u32[]{:S(2)}) copy-start(s32[16]{0:T(128)} %param.9) | copy-start | bytes 196
  51.7 41.4 %all-to-all-start.2 = ((bf16[8,4,192,256]{3,2,1,0:T(8,128)(2,1)}), bf16[8,4,192,256]{3,2,1,0:T(8,128)(2,1)S(1)}, u32[]{:S(2)}, u32[]{:S(2)}) async-start(bf16[8,4,192,256]{3,2,1,0:T(8,128)(2,1)} %shard_map.87), calls=%async_computation.2 | async-start | bytes 6291456 | tf_op jit(solution)/shard_map/all_to_all | solution.py:280
  59.7 64.4 %collective-permute-start.19 = (bf16[2,2,4,192,256]{4,3,2,1,0:T(8,128)(2,1)}, bf16[2,2,4,192,256]{4,3,2,1,0:T(8,128)(2,1)}, u32[]{:S(2)}, u32[]{:S(2)}) collective-permute-start(bf16[2,2,4,192,256]{4,3,2,1,0:T(8,128)(2,1)} %get-tuple-element.50), channel_id=1, source_target_pairs={{4,0},{8,4},{12,8},{5,1},{9,5},{13,9},{6,2},{10,6},{14,10},{7,3},{... | collective-permute-start | bytes 4718600 | tf_op jit(solution)/shard_map/ppermute | solution.py:135
  61.2 65.7 %collective-permute-start.17 = (bf16[2,2,4,192,256]{4,3,2,1,0:T(8,128)(2,1)}, bf16[2,2,4,192,256]{4,3,2,1,0:T(8,128)(2,1)}, u32[]{:S(2)}, u32[]{:S(2)}) collective-permute-start(bf16[2,2,4,192,256]{4,3,2,1,0:T(8,128)(2,1)} %get-tuple-element.51), channel_id=1, source_target_pairs={{0,4},{4,8},{8,12},{1,5},{5,9},{9,13},{2,6},{6,10},{10,14},{3,7},{... | collective-permute-start | bytes 4718600 | tf_op jit(solution)/shard_map/ppermute | solution.py:127
  75.9 41.0 %collective-permute-start.18 = (bf16[1,2,4,192,256]{4,3,2,1,0:T(8,128)(2,1)}, bf16[1,2,4,192,256]{4,3,2,1,0:T(8,128)(2,1)}, u32[]{:S(2)}, u32[]{:S(2)}) collective-permute-start(bf16[1,2,4,192,256]{4,3,2,1,0:T(8,128)(2,1)} %get-tuple-element.48), channel_id=1, source_target_pairs={{0,12},{1,13},{2,14},{3,15},{16,28},{17,29},{18,30},{19,31}} | collective-permute-start | bytes 2359304 | tf_op jit(solution)/shard_map/ppermute | solution.py:136
  93.1 10.7 %copy-start = (bf16[8,4,192,256]{3,2,1,0:T(8,128)(2,1)}, bf16[8,4,192,256]{3,2,1,0:T(8,128)(2,1)S(1)}, u32[]{:S(2)}) copy-start(bf16[8,4,192,256]{3,2,1,0:T(8,128)(2,1)S(1)} %all-to-all-done.2) | copy-start | bytes 9437188
  93.1 75.5 %all-to-all-start = ((bf16[8,4,192,256]{3,2,1,0:T(8,128)(2,1)}), bf16[8,4,192,256]{3,2,1,0:T(8,128)(2,1)}, u32[]{:S(2)}, u32[]{:S(2)}) async-start(bf16[8,4,192,256]{3,2,1,0:T(8,128)(2,1)} %shard_map.84), calls=%async_computation | async-start | bytes 6291456 | tf_op jit(solution)/shard_map/all_to_all | solution.py:280
  99.3 27.7 %collective-permute-start.16 = (bf16[1,2,4,192,256]{4,3,2,1,0:T(8,128)(2,1)}, bf16[1,2,4,192,256]{4,3,2,1,0:T(8,128)(2,1)S(1)}, u32[]{:S(2)}, u32[]{:S(2)}) collective-permute-start(bf16[1,2,4,192,256]{4,3,2,1,0:T(8,128)(2,1)} %get-tuple-element.49), channel_id=1, source_target_pairs={{12,0},{13,1},{14,2},{15,3},{28,16},{29,17},{30,18},{31,19}} | collective-permute-start | bytes 2359304 | tf_op jit(solution)/shard_map/ppermute | solution.py:128
  102.5 70.1 %collective-permute-start.11 = (bf16[2,2,4,192,256]{4,3,2,1,0:T(8,128)(2,1)}, bf16[2,2,4,192,256]{4,3,2,1,0:T(8,128)(2,1)}, u32[]{:S(2)}, u32[]{:S(2)}) collective-permute-start(bf16[2,2,4,192,256]{4,3,2,1,0:T(8,128)(2,1)} %get-tuple-element.54), channel_id=1, source_target_pairs={{4,0},{8,4},{12,8},{5,1},{9,5},{13,9},{6,2},{10,6},{14,10},{7,3},{... | collective-permute-start | bytes 4718600 | tf_op jit(solution)/shard_map/ppermute | solution.py:135
  116.9 43.9 %collective-permute-start.10 = (bf16[1,2,4,192,256]{4,3,2,1,0:T(8,128)(2,1)S(1)}, bf16[1,2,4,192,256]{4,3,2,1,0:T(8,128)(2,1)}, u32[]{:S(2)}, u32[]{:S(2)}) collective-permute-start(bf16[1,2,4,192,256]{4,3,2,1,0:T(8,128)(2,1)S(1)} %get-tuple-element.52), channel_id=1, source_target_pairs={{0,12},{1,13},{2,14},{3,15},{16,28},{17,29},{18,30},{19,31}} | collective-permute-start | bytes 2359304 | tf_op jit(solution)/shard_map/ppermute | solution.py:136
  150.4 93.1 %collective-permute-start.23 = (bf16[2,2,4,192,256]{4,3,2,1,0:T(8,128)(2,1)S(1)}, bf16[2,2,4,192,256]{4,3,2,1,0:T(8,128)(2,1)}, u32[]{:S(2)}, u32[]{:S(2)}) collective-permute-start(bf16[2,2,4,192,256]{4,3,2,1,0:T(8,128)(2,1)S(1)} %get-tuple-element.29), channel_id=1, source_target_pairs={{4,0},{8,4},{12,8},{5,1},{9,5},{13,9},{6,2},{10,6},{14,10},{7,3},{... | collective-permute-start | bytes 4718600 | tf_op jit(solution)/shard_map/ppermute | solution.py:135
  151.7 104.5 %collective-permute-start.21 = (bf16[2,2,4,192,256]{4,3,2,1,0:T(8,128)(2,1)S(1)}, bf16[2,2,4,192,256]{4,3,2,1,0:T(8,128)(2,1)}, u32[]{:S(2)}, u32[]{:S(2)}) collective-permute-start(bf16[2,2,4,192,256]{4,3,2,1,0:T(8,128)(2,1)S(1)} %get-tuple-element.28), channel_id=1, source_target_pairs={{0,4},{4,8},{8,12},{1,5},{5,9},{9,13},{2,6},{6,10},{10,14},{3,7},{... | collective-permute-start | bytes 4718600 | tf_op jit(solution)/shard_map/ppermute | solution.py:127
  157.4 111.2 %collective-permute-start.9 = (bf16[2,2,4,192,256]{4,3,2,1,0:T(8,128)(2,1)}, bf16[2,2,4,192,256]{4,3,2,1,0:T(8,128)(2,1)}, u32[]{:S(2)}, u32[]{:S(2)}) collective-permute-start(bf16[2,2,4,192,256]{4,3,2,1,0:T(8,128)(2,1)} %get-tuple-element.55), channel_id=1, source_target_pairs={{0,4},{4,8},{8,12},{1,5},{5,9},{9,13},{2,6},{6,10},{10,14},{3,7},{... | collective-permute-start | bytes 4718600 | tf_op jit(solution)/shard_map/ppermute | solution.py:127
  160.8 78.5 %collective-permute-start.22 = (bf16[1,2,4,192,256]{4,3,2,1,0:T(8,128)(2,1)}, bf16[1,2,4,192,256]{4,3,2,1,0:T(8,128)(2,1)}, u32[]{:S(2)}, u32[]{:S(2)}) collective-permute-start(bf16[1,2,4,192,256]{4,3,2,1,0:T(8,128)(2,1)} %slice.81), channel_id=1, source_target_pairs={{0,12},{1,13},{2,14},{3,15},{16,28},{17,29},{18,30},{19,31}} | collective-permute-start | bytes 2359304 | tf_op jit(solution)/shard_map/ppermute | solution.py:136
  172.6 75.2 %collective-permute-start.20 = (bf16[1,2,4,192,256]{4,3,2,1,0:T(8,128)(2,1)S(1)}, bf16[1,2,4,192,256]{4,3,2,1,0:T(8,128)(2,1)S(1)}, u32[]{:S(2)}, u32[]{:S(2)}) collective-permute-start(bf16[1,2,4,192,256]{4,3,2,1,0:T(8,128)(2,1)S(1)} %slice.80), channel_id=1, source_target_pairs={{12,0},{13,1},{14,2},{15,3},{28,16},{29,17},{30,18},{31,19}} | collective-permute-start | bytes 2359304 | tf_op jit(solution)/shard_map/ppermute | solution.py:128
  239.4 29.2 %collective-permute-start.8 = (bf16[1,2,4,192,256]{4,3,2,1,0:T(8,128)(2,1)}, bf16[1,2,4,192,256]{4,3,2,1,0:T(8,128)(2,1)}, u32[]{:S(2)}, u32[]{:S(2)}) collective-permute-start(bf16[1,2,4,192,256]{4,3,2,1,0:T(8,128)(2,1)} %get-tuple-element.53), channel_id=1, source_target_pairs={{12,0},{13,1},{14,2},{15,3},{28,16},{29,17},{30,18},{31,19}} | collective-permute-start | bytes 2359304 | tf_op jit(solution)/shard_map/ppermute | solution.py:128
  243.5 65.8 %collective-permute-start.3 = (bf16[2,2,4,192,256]{4,3,2,1,0:T(8,128)(2,1)}, bf16[2,2,4,192,256]{4,3,2,1,0:T(8,128)(2,1)}, u32[]{:S(2)}, u32[]{:S(2)}) collective-permute-start(bf16[2,2,4,192,256]{4,3,2,1,0:T(8,128)(2,1)} %get-tuple-element.58), channel_id=1, source_target_pairs={{4,0},{8,4},{12,8},{5,1},{9,5},{13,9},{6,2},{10,6},{14,10},{7,3},{... | collective-permute-start | bytes 4718600 | tf_op jit(solution)/shard_map/ppermute | solution.py:135
  247.8 59.0 %collective-permute-start.2 = (bf16[1,2,4,192,256]{4,3,2,1,0:T(8,128)(2,1)}, bf16[1,2,4,192,256]{4,3,2,1,0:T(8,128)(2,1)}, u32[]{:S(2)}, u32[]{:S(2)}) collective-permute-start(bf16[1,2,4,192,256]{4,3,2,1,0:T(8,128)(2,1)} %get-tuple-element.56), channel_id=1, source_target_pairs={{0,12},{1,13},{2,14},{3,15},{16,28},{17,29},{18,30},{19,31}} | collective-permute-start | bytes 2359304 | tf_op jit(solution)/shard_map/ppermute | solution.py:136
  264.9 103.3 %all-to-all-start.5 = ((bf16[8,4,192,256]{3,2,1,0:T(8,128)(2,1)}), bf16[8,4,192,256]{3,2,1,0:T(8,128)(2,1)S(1)}, u32[]{:S(2)}, u32[]{:S(2)}) async-start(bf16[8,4,192,256]{3,2,1,0:T(8,128)(2,1)} %shard_map.92), calls=%async_computation.5 | async-start | bytes 6291456 | tf_op jit(solution)/shard_map/all_to_all | solution.py:287
  293.2 65.0 %collective-permute-start.15 = (bf16[2,2,4,192,256]{4,3,2,1,0:T(8,128)(2,1)S(1)}, bf16[2,2,4,192,256]{4,3,2,1,0:T(8,128)(2,1)S(1)}, u32[]{:S(2)}, u32[]{:S(2)}) collective-permute-start(bf16[2,2,4,192,256]{4,3,2,1,0:T(8,128)(2,1)S(1)} %get-tuple-element.26), channel_id=1, source_target_pairs={{4,0},{8,4},{12,8},{5,1},{9,5},{13,9},{6,2},{10,6},{14,10},{7,3},{... | collective-permute-start | bytes 4718600 | tf_op jit(solution)/shard_map/ppermute | solution.py:135
  294.5 65.1 %collective-permute-start.13 = (bf16[2,2,4,192,256]{4,3,2,1,0:T(8,128)(2,1)S(1)}, bf16[2,2,4,192,256]{4,3,2,1,0:T(8,128)(2,1)S(1)}, u32[]{:S(2)}, u32[]{:S(2)}) collective-permute-start(bf16[2,2,4,192,256]{4,3,2,1,0:T(8,128)(2,1)S(1)} %get-tuple-element.25), channel_id=1, source_target_pairs={{0,4},{4,8},{8,12},{1,5},{5,9},{9,13},{2,6},{6,10},{10,14},{3,7},{... | collective-permute-start | bytes 4718600 | tf_op jit(solution)/shard_map/ppermute | solution.py:127
  302.5 51.5 %collective-permute-start.14 = (bf16[1,2,4,192,256]{4,3,2,1,0:T(8,128)(2,1)S(1)}, bf16[1,2,4,192,256]{4,3,2,1,0:T(8,128)(2,1)S(1)}, u32[]{:S(2)}, u32[]{:S(2)}) collective-permute-start(bf16[1,2,4,192,256]{4,3,2,1,0:T(8,128)(2,1)S(1)} %slice.75), channel_id=1, source_target_pairs={{0,12},{1,13},{2,14},{3,15},{16,28},{17,29},{18,30},{19,31}} | collective-permute-start | bytes 2359304 | tf_op jit(solution)/shard_map/ppermute | solution.py:136
  306.8 80.5 %collective-permute-start.1 = (bf16[2,2,4,192,256]{4,3,2,1,0:T(8,128)(2,1)}, bf16[2,2,4,192,256]{4,3,2,1,0:T(8,128)(2,1)}, u32[]{:S(2)}, u32[]{:S(2)}) collective-permute-start(bf16[2,2,4,192,256]{4,3,2,1,0:T(8,128)(2,1)} %get-tuple-element.59), channel_id=1, source_target_pairs={{0,4},{4,8},{8,12},{1,5},{5,9},{9,13},{2,6},{6,10},{10,14},{3,7},{... | collective-permute-start | bytes 4718600 | tf_op jit(solution)/shard_map/ppermute | solution.py:127
  309.4 50.2 %collective-permute-start.12 = (bf16[1,2,4,192,256]{4,3,2,1,0:T(8,128)(2,1)S(1)}, bf16[1,2,4,192,256]{4,3,2,1,0:T(8,128)(2,1)S(1)}, u32[]{:S(2)}, u32[]{:S(2)}) collective-permute-start(bf16[1,2,4,192,256]{4,3,2,1,0:T(8,128)(2,1)S(1)} %slice.74), channel_id=1, source_target_pairs={{12,0},{13,1},{14,2},{15,3},{28,16},{29,17},{30,18},{31,19}} | collective-permute-start | bytes 2359304 | tf_op jit(solution)/shard_map/ppermute | solution.py:128
  354.0 22.6 %collective-permute-start = (bf16[1,2,4,192,256]{4,3,2,1,0:T(8,128)(2,1)}, bf16[1,2,4,192,256]{4,3,2,1,0:T(8,128)(2,1)}, u32[]{:S(2)}, u32[]{:S(2)}) collective-permute-start(bf16[1,2,4,192,256]{4,3,2,1,0:T(8,128)(2,1)} %get-tuple-element.57), channel_id=1, source_target_pairs={{12,0},{13,1},{14,2},{15,3},{28,16},{29,17},{30,18},{31,19}} | collective-permute-start | bytes 2359304 | tf_op jit(solution)/shard_map/ppermute | solution.py:128
  369.8 117.1 %all-to-all-start.3 = ((bf16[8,4,192,256]{3,2,1,0:T(8,128)(2,1)}), bf16[8,4,192,256]{3,2,1,0:T(8,128)(2,1)}, u32[]{:S(2)}, u32[]{:S(2)}) async-start(bf16[8,4,192,256]{3,2,1,0:T(8,128)(2,1)} %shard_map.89), calls=%async_computation.3 | async-start | bytes 6291456 | tf_op jit(solution)/shard_map/all_to_all | solution.py:287
  411.8 64.7 %collective-permute-start.7 = (bf16[2,2,4,192,256]{4,3,2,1,0:T(8,128)(2,1)S(1)}, bf16[2,2,4,192,256]{4,3,2,1,0:T(8,128)(2,1)S(1)}, u32[]{:S(2)}, u32[]{:S(2)}) collective-permute-start(bf16[2,2,4,192,256]{4,3,2,1,0:T(8,128)(2,1)S(1)} %get-tuple-element.23), channel_id=1, source_target_pairs={{4,0},{8,4},{12,8},{5,1},{9,5},{13,9},{6,2},{10,6},{14,10},{7,3},{... | collective-permute-start | bytes 4718600 | tf_op jit(solution)/shard_map/ppermute | solution.py:135
  413.1 65.1 %collective-permute-start.5 = (bf16[2,2,4,192,256]{4,3,2,1,0:T(8,128)(2,1)S(1)}, bf16[2,2,4,192,256]{4,3,2,1,0:T(8,128)(2,1)S(1)}, u32[]{:S(2)}, u32[]{:S(2)}) collective-permute-start(bf16[2,2,4,192,256]{4,3,2,1,0:T(8,128)(2,1)S(1)} %get-tuple-element.22), channel_id=1, source_target_pairs={{0,4},{4,8},{8,12},{1,5},{5,9},{9,13},{2,6},{6,10},{10,14},{3,7},{... | collective-permute-start | bytes 4718600 | tf_op jit(solution)/shard_map/ppermute | solution.py:127
  426.4 50.1 %collective-permute-start.6 = (bf16[1,2,4,192,256]{4,3,2,1,0:T(8,128)(2,1)S(1)}, bf16[1,2,4,192,256]{4,3,2,1,0:T(8,128)(2,1)S(1)}, u32[]{:S(2)}, u32[]{:S(2)}) collective-permute-start(bf16[1,2,4,192,256]{4,3,2,1,0:T(8,128)(2,1)S(1)} %slice.69), channel_id=1, source_target_pairs={{0,12},{1,13},{2,14},{3,15},{16,28},{17,29},{18,30},{19,31}} | collective-permute-start | bytes 2359304 | tf_op jit(solution)/shard_map/ppermute | solution.py:136
  430.8 47.4 %collective-permute-start.4 = (bf16[1,2,4,192,256]{4,3,2,1,0:T(8,128)(2,1)S(1)}, bf16[1,2,4,192,256]{4,3,2,1,0:T(8,128)(2,1)S(1)}, u32[]{:S(2)}, u32[]{:S(2)}) collective-permute-start(bf16[1,2,4,192,256]{4,3,2,1,0:T(8,128)(2,1)S(1)} %slice.68), channel_id=1, source_target_pairs={{12,0},{13,1},{14,2},{15,3},{28,16},{29,17},{30,18},{31,19}} | collective-permute-start | bytes 2359304 | tf_op jit(solution)/shard_map/ppermute | solution.py:128
  487.0 41.4 %all-to-all-start.1 = ((bf16[8,4,192,256]{3,2,1,0:T(8,128)(2,1)}), bf16[8,4,192,256]{3,2,1,0:T(8,128)(2,1)S(1)}, u32[]{:S(2)}, u32[]{:S(2)}) async-start(bf16[8,4,192,256]{3,2,1,0:T(8,128)(2,1)} %shard_map.86), calls=%async_computation.1 | async-start | bytes 6291456 | tf_op jit(solution)/shard_map/all_to_all | solution.py:287
  (3 other events, 4.9 us)
